TPU v7x, 128 devices: a whole 4x4x4 slice. The times are simulated.
128 devices in a mesh: feat: 64 (over z, x, y), frame: 2 (over core).
Axes of the slice: x: 4, y: 4, z: 4, core: 2. Of those that a mesh axis runs over, the one named last changes fastest.
Arguments:
- frames: float32 [6144, 440], P(('frame', 'feat')), may hold values from -6 to 6
- labels: int32 [6144], P('frame'), may hold values from 0 to 146, as said below
- proj: float32 [440, 131072], P(None, 'feat'), may hold values from -1 to 1
- phase: float32 [131072], P('feat'), may hold values from 0 to 6.2832
- class_weights: float32 [131072, 147], P('feat'), may hold values from -40 to 40
- velocity: float32 [131072, 147], P('feat'), may hold values from -3 to 3
Outputs:
- weights_out: float32 [131072, 147], P('feat')
- velocity_out: float32 [131072, 147], P('feat')
Inputs may be any that keep to these rules, and one draw needn't show every extreme that they name: labels come in runs of 4 to 12 consecutive frames that share one class (phone segments); neighbouring runs may share a class.
All inputs are finite; a program needn't handle non-finite values.
Results may differ from a plain program's by a relative error of at most 0.00011.
Values sent between devices are 32-bit elements; how exact they have to be, the bound alone decides.
A program may use at most 128 MiB of HBM per device.

v0:
```python
import math

import jax
import jax.numpy as jnp
from jax import lax
from jax.sharding import PartitionSpec as P

ITERS = 2


MOMENTUM = 0.9
STEP_RATE = 0.05
EPSILON = 1e-06


def residual_of(scores, onehot):
    row_max = jnp.max(scores, axis=1, keepdims=True)
    exponent = jnp.exp(scores - row_max)
    probability = exponent / jnp.sum(exponent, axis=1, keepdims=True)
    return probability - onehot


def on_device(frames, labels, proj, phase, class_weights, velocity):
    feat_count = lax.axis_size("feat") * proj.shape[1]
    classes = class_weights.shape[1]
    feat_scale = math.sqrt(2.0 / feat_count)
    count_all = feat_count * classes
    angles = jnp.dot(
        lax.all_gather(frames, "feat", axis=0, tiled=True),
        proj,
        precision=lax.Precision.HIGHEST,
        preferred_element_type=jnp.float32,
    )
    features = feat_scale * jnp.cos(angles + phase[None, :])
    onehot = (labels[:, None] == jnp.arange(classes, dtype=jnp.int32)[None, :]).astype(jnp.float32)
    weights_now = class_weights
    velocity_now = velocity
    for iteration in range(ITERS):
        advance = weights_now + MOMENTUM * velocity_now
        partial_value = jnp.dot(
            features, advance, precision=lax.Precision.HIGHEST, preferred_element_type=jnp.float32
        )
        scores = lax.psum(partial_value, "feat")
        residual = residual_of(scores, onehot)
        grad_local = lax.dot_general(
            features,
            residual,
            (((0,), (0,)), ((), ())),
            precision=lax.Precision.HIGHEST,
            preferred_element_type=jnp.float32,
        )
        gradient = lax.psum(grad_local, "frame")
        square_sum = lax.psum(jnp.sum(gradient * gradient), "feat")
        grad_rms = jnp.sqrt(square_sum / count_all + EPSILON)
        velocity_now = MOMENTUM * velocity_now - STEP_RATE * gradient / grad_rms
        weights_now = weights_now + velocity_now
    return (weights_now, velocity_now)


def solution(mesh):
    return jax.shard_map(
        on_device,
        mesh=mesh,
        in_specs=(
            P(("frame", "feat"), None),
            P("frame"),
            P(None, "feat"),
            P("feat"),
            P("feat", None),
            P("feat", None),
        ),
        out_specs=(P("feat", None), P("feat", None)),
        check_vma=False,
    )
```

profile of v0, /device:TPU:0, one launch (start us, length us, event | category | flops | bytes accessed | tf_op | source)
XLA Modules:
  0.0 1248.7 jit_solution(5423682945566969221)
XLA Ops:
  7.2 0.0 all-gather.2.cloned.1.call-start
  7.2 0.7 all-gather.2.cloned.1.call-update
  7.9 0.0 all-reduce.5.cloned.1.call-start
  7.9 1.8 fusion.38
  9.8 0.0 copy-start.6
  9.8 75.3 %all-gather.2.cloned.1.call-done = f32[3072,440]{1,0:T(8,128)} async-done(((f32[48,440]{1,0:T(8,128)}), f32[3072,440]{1,0:T(8,128)}) %all-gather.2.cloned.1.call-update) | async-done | bytes 5406736 | tf_op jit(solution)/shard_map/all_gather | solution.py:29
  85.1 44.6 %fusion.28 = f32[3072,2048]{1,0:T(8,128)S(1)} fusion(f32[3072,440]{1,0:T(8,128)} %all-gather.2.cloned.1.call-done, f32[440,2048]{1,0:T(8,128)} %param.8), kind=kOutput, calls=%fused_computation.38 | convolution fusion | flops 33218887680 | bytes 34177024 | tf_op jit(solution)/shard_map/dot_general | solution.py:28
  129.7 0.0 copy-start
  129.8 8.3 copy-done
  138.1 0.0 copy-done.6
  138.1 116.2 %fusion.3 = f32[3072,147]{0,1:T(8,128)} fusion(f32[3072,2048]{1,0:T(8,128)S(1)} %fusion.28, f32[2048]{0:T(1024)S(1)} %copy-done.6, f32[2048,147]{0,1:T(8,128)S(1)} %fusion.38), kind=kOutput, calls=%fused_computation.4 | convolution fusion | flops 11110711296 | bytes 28184576 | tf_op jit(solution)/shard_map/dot_general | solution.py:40
  254.2 0.0 all-reduce.5.cloned.1.call-update
  254.3 0.0 copy-start.7
  254.3 0.0 all-reduce.7.cloned.1.call-start
  254.3 131.7 %all-reduce.5.cloned.1.call-done = f32[3072,147]{0,1:T(8,128)} async-done(((f32[3072,147]{0,1:T(8,128)}), f32[3072,147]{0,1:T(8,128)}) %all-reduce.5.cloned.1.call-update) | async-done | bytes 1806352 | tf_op jit(solution)/shard_map/psum | solution.py:43
  386.1 0.0 copy-start.2
  386.1 1.7 reduce_max.18
  387.8 0.3 copy-done.2
  388.1 0.3 fusion.6
  388.4 0.0 copy-done.7
  388.4 0.4 convert_subtract_fusion.11
  388.9 99.3 %fusion.2 = f32[2048,147]{0,1:T(8,128)} fusion(f32[3072,2048]{1,0:T(8,128)} %copy-done, f32[2048]{0:T(1024)S(1)} %copy-done.6, f32[3072,147]{0,1:T(8,128)S(1)} %convert_subtract_fusion.11), kind=kOutput, calls=%fused_computation.3 | convolution fusion | flops 11110711296 | bytes 28184576 | tf_op jit(solution)/shard_map/dot_general | solution.py:45
  488.1 0.0 copy-start.5
  488.1 0.0 all-reduce.7.cloned.1.call-update
  488.2 0.0 all-reduce.9.cloned.1.call-start
  488.2 23.0 %all-reduce.7.cloned.1.call-done = f32[2048,147]{0,1:T(8,128)} async-done(((f32[2048,147]{0,1:T(8,128)}), f32[2048,147]{0,1:T(8,128)}) %all-reduce.7.cloned.1.call-update) | async-done | bytes 1204240 | tf_op jit(solution)/shard_map/psum | solution.py:52
  511.2 2.2 multiply_reduce_fusion.1
  513.4 179.7 %psum.44 = f32[]{:T(128)} all-reduce(f32[]{:T(128)} %multiply_reduce_fusion.1), channel_id=1, replica_groups=mesh['feat'=64,'frame'=2] {'feat'}, use_global_device_ids=true, to_apply=%region_5.0 | all-reduce | flops 1 | bytes 8 | tf_op jit(solution)/shard_map/psum | solution.py:53
  693.8 0.0 copy-done.5
  693.8 2.0 fusion.27
  695.8 0.0 copy-start.3
  695.8 0.2 fusion.35
  696.0 0.8 copy-done.3
  696.8 108.2 %fusion.1 = f32[3072,147]{0,1:T(8,128)} fusion(f32[3072,2048]{1,0:T(8,128)} %copy-done, f32[2048]{0:T(1024)S(1)} %copy-done.6, f32[2048,147]{0,1:T(8,128)S(1)} %fusion.35), kind=kOutput, calls=%fused_computation.2 | convolution fusion | flops 11110711296 | bytes 28184576 | tf_op jit(solution)/shard_map/dot_general | solution.py:40
  805.1 0.0 all-reduce.9.cloned.1.call-update
  805.1 0.0 all-reduce.11.cloned.1.call-start
  805.2 125.8 %all-reduce.9.cloned.1.call-done = f32[3072,147]{0,1:T(8,128)} async-done(((f32[3072,147]{0,1:T(8,128)}), f32[3072,147]{0,1:T(8,128)}) %all-reduce.9.cloned.1.call-update) | async-done | bytes 1806352 | tf_op jit(solution)/shard_map/psum | solution.py:43
  931.0 0.0 copy-start.1
  931.0 1.8 reduce_max.19
  932.7 0.3 copy-done.1
  933.0 0.3 fusion.7
  933.3 0.4 convert_subtract_fusion.10
  933.8 99.3 %fusion = f32[2048,147]{0,1:T(8,128)} fusion(f32[3072,2048]{1,0:T(8,128)} %copy-done, f32[2048]{0:T(1024)S(1)} %copy-done.6, f32[3072,147]{0,1:T(8,128)S(1)} %convert_subtract_fusion.10), kind=kOutput, calls=%fused_computation.1 | convolution fusion | flops 11110711296 | bytes 28184576 | tf_op jit(solution)/shard_map/dot_general | solution.py:45
  1033.1 0.0 copy-start.4
  1033.1 0.0 all-reduce.11.cloned.1.call-update
  1033.1 23.0 %all-reduce.11.cloned.1.call-done = f32[2048,147]{0,1:T(8,128)} async-done(((f32[2048,147]{0,1:T(8,128)}), f32[2048,147]{0,1:T(8,128)}) %all-reduce.11.cloned.1.call-update) | async-done | bytes 1204240 | tf_op jit(solution)/shard_map/psum | solution.py:52
  1056.1 2.2 multiply_reduce_fusion
  1058.4 179.7 %psum.47 = f32[]{:T(128)} all-reduce(f32[]{:T(128)} %multiply_reduce_fusion), channel_id=1, replica_groups=mesh['feat'=64,'frame'=2] {'feat'}, use_global_device_ids=true, to_apply=%region_11.0 | all-reduce | flops 1 | bytes 8 | tf_op jit(solution)/shard_map/psum | solution.py:53
  1238.8 0.0 copy-done.4
  1238.8 3.1 fusion.26
Async XLA Ops:
  7.2 77.9 %all-gather.2.cloned.1.call-start = ((), (), s32[]{:S(2)}) async-start(), calls=%async_computation | async-start | bytes 6389760 | tf_op jit(solution)/shard_map/all_gather | solution.py:29
  7.9 378.2 %all-reduce.5.cloned.1.call-start = ((), (), s32[]{:S(2)}) async-start(), calls=%async_computation.1 | async-start | bytes 3735552 | tf_op jit(solution)/shard_map/psum | solution.py:43
  9.8 128.3 %copy-start.6 = (f32[2048]{0:T(1024)S(1)}, f32[2048]{0:T(1024)}, u32[]{:S(2)}) copy-start(f32[2048]{0:T(1024)} %param.9) | copy-start | bytes 24580
  129.7 8.3 copy-start
  254.3 134.1 %copy-start.7 = (s32[3072]{0:T(1024)S(1)}, s32[3072]{0:T(1024)}, u32[]{:S(2)}) copy-start(s32[3072]{0:T(1024)} %param.7) | copy-start | bytes 36868
  254.3 256.9 %all-reduce.7.cloned.1.call-start = ((), (), s32[]{:S(2)}) async-start(), calls=%async_computation.2 | async-start | bytes 2490368 | tf_op jit(solution)/shard_map/psum | solution.py:52
  386.1 2.1 copy-start.2
  488.1 205.7 %copy-start.5 = (f32[2048,147]{0,1:T(8,128)S(1)}, f32[2048,147]{0,1:T(8,128)}, u32[]{:S(2)}) copy-start(f32[2048,147]{0,1:T(8,128)} %param.10) | copy-start | bytes 3612676
  488.2 442.8 %all-reduce.9.cloned.1.call-start = ((), (), s32[]{:S(2)}) async-start(), calls=%async_computation.3 | async-start | bytes 3735552 | tf_op jit(solution)/shard_map/psum | solution.py:43
  695.8 1.0 copy-start.3
  805.1 251.0 %all-reduce.11.cloned.1.call-start = ((), (), s32[]{:S(2)}) async-start(), calls=%async_computation.4 | async-start | bytes 2490368 | tf_op jit(solution)/shard_map/psum | solution.py:52
  931.0 2.1 copy-start.1
  1033.1 205.7 %copy-start.4 = (f32[2048,147]{0,1:T(8,128)S(1)}, f32[2048,147]{0,1:T(8,128)}, u32[]{:S(2)}) copy-start(f32[2048,147]{0,1:T(8,128)} %copy-done.3) | copy-start | bytes 3612676
Sparse Core Ops, SparseCore 0:
  10.7 74.3 all-gather.1
  254.4 131.6 all-reduce.4
  488.3 22.8 all-reduce.6
  805.2 125.6 all-reduce.8
  1033.2 22.8 all-reduce.10
where the time goes:
time: 1260 us; the launch traced here: 1250 us
  matrix products  468 us (37%)
  waiting for transfers between devices  380 us (30%)
  blocking collectives  359 us (28%)
  other arithmetic  16.4 us (1%)
  between operations  15.7 us (1%)
    psum x2, blocking collectives, on_device(): square_sum = lax.psum(jnp.sum(gradient * gradient), 'feat')  359 us
    psum x2, waiting for transfers between devices, on_device(): scores = lax.psum(partial_value, 'feat')  258 us
    dot_general x2, matrix products, on_device(): jnp.dot(features, advance, precision=lax.Precision.HIGHEST, preferred_ele...  224 us
    dot_general x2, matrix products, on_device(): lax.dot_general(features, residual, (((0,), (0,)), ((), ())), precision=l...  199 us
    all_gather x1, waiting for transfers between devices, on_device(): lax.all_gather(frames, 'feat', axis=0, tiled=True)  75.3 us
    psum x2, waiting for transfers between devices, on_device(): gradient = lax.psum(grad_local, 'frame')  46 us
    dot_general x1, matrix products, on_device(): jnp.dot(lax.all_gather(frames, 'feat', axis=0, tiled=True), proj, precisi...  44.6 us
  transfers between devices with their start and end apart: 5, of which 5 were waited for; matrix products, arithmetic and copies ran while one was open for 0% of the time, Pallas kernels for 0%

commit v1 on v0

v1 whole, which is shorter than its diff:
```python
import functools
import math

import jax
import jax.numpy as jnp
from jax import lax
from jax.experimental import pallas as pl
from jax.experimental.pallas import tpu as pltpu
from jax.sharding import PartitionSpec as P

MOMENTUM = 0.9
STEP_RATE = 0.05
EPSILON = 1e-06
TURN = 1.0 / (2.0 * math.pi)
ROUNDER = 1.5 * 2.0**23
SINE = (
    6.283185160089458,
    -41.34165503141172,
    81.60100407300267,
    -76.54978228814288,
    39.53670602749812,
)
MESH = pl.DeviceIdType.MESH
VMEM_LIMIT = 60 * 2**20
CLASS_PAD = 160
UNIT = CLASS_PAD // 2


def positions():
    index = lax.axis_index("feat")
    return {"z": index // 16, "x": (index // 4) % 4, "y": index % 4}


def feat_at(pos, dim, step):
    moved = dict(pos)
    moved[dim] = (pos[dim] + step) % 4
    return moved["z"] * 16 + moved["x"] * 4 + moved["y"]


class Copies:
    def __init__(self, send_sems, recv_sems):
        self.send_sems, self.recv_sems, self.made = send_sems, recv_sems, []

    def send(self, src, dst, device):
        slot = len(self.made)
        copy = pltpu.make_async_remote_copy(
            src_ref=src,
            dst_ref=dst,
            send_sem=self.send_sems.at[slot],
            recv_sem=self.recv_sems.at[slot],
            device_id=device,
            device_id_type=MESH,
        )
        copy.start()
        self.made.append(copy)
        return copy

    def wait_sends(self):
        for copy in self.made:
            copy.wait_send()


def greet(devices):
    barrier = pltpu.get_barrier_semaphore()
    for device in devices:
        pl.semaphore_signal(barrier, inc=1, device_id=device, device_id_type=MESH)
    pl.semaphore_wait(barrier, len(devices))


def gather_ring(copies, pos, dim, source, block):
    here = pos[dim]
    right = {"feat": feat_at(pos, dim, 1)}
    left = {"feat": feat_at(pos, dim, 3)}
    before, after = (here + 3) % 4, (here + 1) % 4
    first_right = copies.send(source(0), block(here, 0), right)
    first_left = copies.send(source(1), block(here, 1), left)
    second_right = copies.send(source(1), block(here, 1), right)
    second_left = copies.send(source(0), block(here, 0), left)
    yield
    first_right.wait_recv()
    on_right = copies.send(block(before, 0), block(before, 0), right)
    first_left.wait_recv()
    on_left = copies.send(block(after, 1), block(after, 1), left)
    yield
    for copy in (second_right, second_left, on_right, on_left):
        copy.wait_recv()


def run_all(streams):
    streams = list(streams)
    while streams:
        alive = []
        for stream in streams:
            try:
                next(stream)
                alive.append(stream)
            except StopIteration:
                pass
        streams = alive


COLOURS = (("y", "x", "z"), ("x", "z", "y"), ("z", "y", "x"))
FRAME_COPIES = 3 * 3 * 6
SCORE_COPIES = 3 * (6 + 6 + 3 + 6 + 6)


def frames_kernel(x_ref, out_ref, send_sems, recv_sems, local_sem):
    pos = positions()
    greet([{"feat": feat_at(pos, dim, step)} for dim in "zxy" for step in (1, 3)])
    copies = Copies(send_sems, recv_sems)
    own = pltpu.make_async_copy(x_ref, out_ref.at[pos["z"], pos["x"], pos["y"]], local_sem)
    own.start()
    state = {"own": False}
    third = x_ref.shape[0] // 3
    half = third // 2

    def colour(c, dims):
        done = []
        for dim in dims:

            def block(q, h, dim=dim, done=tuple(done)):
                index = tuple(
                    slice(None) if name in done else (q if name == dim else pos[name])
                    for name in "zxy"
                )
                return out_ref.at[index + (pl.ds(third * c + half * h, half),)]

            def source(h, block=block, dim=dim, first=not done):
                if first:
                    return x_ref.at[pl.ds(third * c + half * h, half)]
                return block(pos[dim], h)

            yield from gather_ring(copies, pos, dim, source, block)
            if not state["own"]:
                own.wait()
                state["own"] = True
            done.append(dim)
            yield

    run_all([colour(c, dims) for c, dims in enumerate(COLOURS)])
    copies.wait_sends()


def gather_frames(frames):
    rows, width = frames.shape
    return pl.pallas_call(
        frames_kernel,
        out_shape=jax.ShapeDtypeStruct((4, 4, 4, rows, width), jnp.float32),
        in_specs=[pl.BlockSpec(memory_space=pl.ANY)],
        out_specs=pl.BlockSpec(memory_space=pl.ANY),
        scratch_shapes=[
            pltpu.SemaphoreType.DMA((FRAME_COPIES,)),
            pltpu.SemaphoreType.DMA((FRAME_COPIES,)),
            pltpu.SemaphoreType.DMA,
        ],
        compiler_params=pltpu.CompilerParams(collective_id=0, has_side_effects=True),
        name="gather_frames",
    )(frames)


def scores_kernel(
    p_ref, out_ref, total, from_left, from_right, onward_r, onward_l, sum_left, sum_right, kept,
    small_left, small_right, small_r, small_l, unit_left, unit_right, unit, others,
    send_sems, recv_sems,
):
    pos = positions()
    greet([{"feat": feat_at(pos, dim, step)} for dim in "zxy" for step in (1, 2, 3)])
    copies = Copies(send_sems, recv_sems)
    half = UNIT // 2

    def colour(c, dims):
        d1, d2, d3 = dims
        a, b = pos[d1], pos[d2]
        base = 16 * c

        def part(i, h):
            return pl.ds(base + 4 * i + 2 * h, 2)

        right, left = {"feat": feat_at(pos, d1, 1)}, {"feat": feat_at(pos, d1, 3)}
        far, after, before = (a + 2) % 4, (a + 1) % 4, (a + 3) % 4
        s1 = copies.send(p_ref.at[part(far, 0)], from_left.at[c], right)
        s2 = copies.send(p_ref.at[part(far, 1)], from_right.at[c], left)
        s3 = copies.send(p_ref.at[part(after, 1)], sum_left.at[c, 1], right)
        s4 = copies.send(p_ref.at[part(before, 0)], sum_right.at[c, 0], left)
        yield
        s1.wait_recv()
        onward_r[c] = p_ref[part(after, 0)] + from_left[c]
        s5 = copies.send(onward_r.at[c], sum_left.at[c, 0], right)
        s2.wait_recv()
        onward_l[c] = p_ref[part(before, 1)] + from_right[c]
        s6 = copies.send(onward_l.at[c], sum_right.at[c, 1], left)
        yield
        for copy in (s3, s4, s5, s6):
            copy.wait_recv()
        for h in range(2):
            kept[c, pl.ds(2 * h, 2)] = p_ref[part(a, h)] + (sum_left[c, h] + sum_right[c, h])

        right, left = {"feat": feat_at(pos, d2, 1)}, {"feat": feat_at(pos, d2, 3)}
        far, after, before = (b + 2) % 4, (b + 1) % 4, (b + 3) % 4
        low, high = pl.ds(0, half), pl.ds(half, half)
        s1 = copies.send(kept.at[c, far, low], small_left.at[c], right)
        s2 = copies.send(kept.at[c, far, high], small_right.at[c], left)
        s3 = copies.send(kept.at[c, after, high], unit_left.at[c, 1], right)
        s4 = copies.send(kept.at[c, before, low], unit_right.at[c, 0], left)
        yield
        s1.wait_recv()
        small_r[c] = kept[c, after, low] + small_left[c]
        s5 = copies.send(small_r.at[c], unit_left.at[c, 0], right)
        s2.wait_recv()
        small_l[c] = kept[c, before, high] + small_right[c]
        s6 = copies.send(small_l.at[c], unit_right.at[c, 1], left)
        yield
        for copy in (s3, s4, s5, s6):
            copy.wait_recv()
        for h, rows in enumerate((low, high)):
            unit[c, rows] = kept[c, b, rows] + (unit_left[c, h] + unit_right[c, h])

        parts = [
            copies.send(unit.at[c], others.at[c, slot], {"feat": feat_at(pos, d3, step)})
            for slot, step in enumerate((2, 1, 3))
        ]
        yield
        for copy in parts:
            copy.wait_recv()
        total[base + 4 * a + b] = (unit[c] + others[c, 0]) + (others[c, 1] + others[c, 2])

        def unit_block(q, h):
            return total.at[base + 4 * a + q, pl.ds(half * h, half)]

        yield from gather_ring(copies, pos, d2, lambda h: unit_block(b, h), unit_block)

        def row_block(q, h):
            return total.at[part(q, h)]

        yield from gather_ring(copies, pos, d1, lambda h: row_block(a, h), row_block)

    run_all([colour(c, dims) for c, dims in enumerate(COLOURS)])

    def put(u, carry):
        out_ref[u] = total[u]
        return carry

    lax.fori_loop(0, total.shape[0], put, 0)
    copies.wait_sends()


def sum_scores(partial_scores, collective_id):
    units = partial_scores.shape[0]
    f32 = jnp.float32
    half = UNIT // 2
    return pl.pallas_call(
        scores_kernel,
        out_shape=jax.ShapeDtypeStruct(partial_scores.shape, f32),
        in_specs=[pl.BlockSpec(memory_space=pltpu.VMEM)],
        out_specs=pl.BlockSpec(memory_space=pltpu.VMEM),
        scratch_shapes=[
            pltpu.VMEM((units, UNIT, 128), f32),
            pltpu.VMEM((3, 2, UNIT, 128), f32),
            pltpu.VMEM((3, 2, UNIT, 128), f32),
            pltpu.VMEM((3, 2, UNIT, 128), f32),
            pltpu.VMEM((3, 2, UNIT, 128), f32),
            pltpu.VMEM((3, 2, 2, UNIT, 128), f32),
            pltpu.VMEM((3, 2, 2, UNIT, 128), f32),
            pltpu.VMEM((3, 4, UNIT, 128), f32),
            pltpu.VMEM((3, half, 128), f32),
            pltpu.VMEM((3, half, 128), f32),
            pltpu.VMEM((3, half, 128), f32),
            pltpu.VMEM((3, half, 128), f32),
            pltpu.VMEM((3, 2, half, 128), f32),
            pltpu.VMEM((3, 2, half, 128), f32),
            pltpu.VMEM((3, UNIT, 128), f32),
            pltpu.VMEM((3, 3, UNIT, 128), f32),
            pltpu.SemaphoreType.DMA((SCORE_COPIES,)),
            pltpu.SemaphoreType.DMA((SCORE_COPIES,)),
        ],
        compiler_params=pltpu.CompilerParams(
            collective_id=collective_id, has_side_effects=True, vmem_limit_bytes=VMEM_LIMIT
        ),
        name=f"sum_scores_{collective_id}",
    )(partial_scores)


def split(value):
    high = value.astype(jnp.bfloat16)
    return high, (value - high.astype(jnp.float32)).astype(jnp.bfloat16)


def mul(left, right):
    return jnp.dot(left, right, preferred_element_type=jnp.float32)


def load_advance(w_ref, v_ref, a_high, a_low, scale):
    classes = w_ref.shape[1]
    a_high[...] = jnp.zeros_like(a_high)
    a_low[...] = jnp.zeros_like(a_low)
    rows = 256

    def part(i, carry):
        at = pl.ds(pl.multiple_of(i * rows, rows), rows)
        high, low = split((w_ref[at, :] + MOMENTUM * v_ref[at, :]) * scale)
        a_high[at, :classes] = high
        a_low[at, :classes] = low
        return carry

    lax.fori_loop(0, w_ref.shape[0] // rows, part, 0)


def put_scores(out_ref, scores):
    flipped = scores.T
    for k in range(scores.shape[0] // 128):
        out_ref[k] = flipped[:CLASS_PAD, 128 * k : 128 * (k + 1)]


def features_kernel(
    scale, x_ref, proj_ref, phase_ref, w_ref, v_ref, high_ref, low_ref, out_ref,
    x_pad, proj_pad, p_high, p_low, a_high, a_low,
):
    depth = x_ref.shape[1]
    padded = x_pad.shape[1]
    width = proj_ref.shape[1]

    @pl.when(pl.program_id(0) == 0)
    def _():
        load_advance(w_ref, v_ref, a_high, a_low, scale)
        proj_pad[...] = jnp.zeros_like(proj_pad)
        proj_pad[:depth, :] = proj_ref[...] * TURN
        phase = phase_ref[...] * TURN
        top = phase.astype(jnp.bfloat16).astype(jnp.float32)
        row = lax.broadcasted_iota(jnp.int32, (8, width), 0)
        proj_pad[depth : depth + 8, :] = jnp.where(
            row == 0, top, jnp.where(row == 1, phase - top, 0.0)
        )
        step = 64
        for k in range(padded // step):
            at = pl.ds(k * step, step)
            p_high[at, :], p_low[at, :] = split(proj_pad[at, :])
        lane = lax.broadcasted_iota(jnp.int32, x_pad.shape, 1)
        x_pad[...] = jnp.where((lane == depth) | (lane == depth + 1), 1.0, 0.0)

    x_pad[:, :depth] = x_ref[...]
    x_high, x_low = split(x_pad[...])
    tile = 256
    for n in range(width // tile):
        at = pl.ds(n * tile, tile)
        turns = mul(x_high, p_high[:, at]) + mul(x_high, p_low[:, at]) + mul(x_low, p_high[:, at])
        turns = turns - ((turns + ROUNDER) - ROUNDER)
        quarter = 0.25 - jnp.abs(turns)
        square = quarter * quarter
        value = SINE[4]
        for coefficient in SINE[3::-1]:
            value = value * square + coefficient
        high_ref[:, at], low_ref[:, at] = split(value * quarter)
    high, low = high_ref[...], low_ref[...]
    put_scores(
        out_ref, mul(high, a_high[...]) + mul(high, a_low[...]) + mul(low, a_high[...])
    )


def make_features(frames, proj, phase, weights, velocity, scale):
    count, depth = frames.shape
    width, classes = weights.shape
    block = 256
    padded = 512
    bf16 = jnp.bfloat16
    whole = lambda shape: pl.BlockSpec(shape, lambda i: (0, 0), pipeline_mode=pl.Buffered(1))
    return pl.pallas_call(
        functools.partial(features_kernel, scale),
        grid=(count // block,),
        out_shape=[
            jax.ShapeDtypeStruct((count, width), bf16),
            jax.ShapeDtypeStruct((count, width), bf16),
            jax.ShapeDtypeStruct((count // 128, CLASS_PAD, 128), jnp.float32),
        ],
        in_specs=[
            pl.BlockSpec((block, depth), lambda i: (i, 0)),
            whole((depth, width)),
            whole((1, width)),
            whole((width, classes)),
            whole((width, classes)),
        ],
        out_specs=[
            pl.BlockSpec((block, width), lambda i: (i, 0)),
            pl.BlockSpec((block, width), lambda i: (i, 0)),
            pl.BlockSpec((block // 128, CLASS_PAD, 128), lambda i: (i, 0, 0)),
        ],
        scratch_shapes=[
            pltpu.VMEM((block, padded), jnp.float32),
            pltpu.VMEM((padded, width), jnp.float32),
            pltpu.VMEM((padded, width), bf16),
            pltpu.VMEM((padded, width), bf16),
            pltpu.VMEM((width, 256), bf16),
            pltpu.VMEM((width, 256), bf16),
        ],
        compiler_params=pltpu.CompilerParams(vmem_limit_bytes=VMEM_LIMIT),
        name="make_features",
    )(frames, proj, phase.reshape(1, width), weights, velocity)


def rescore_kernel(scale, high_ref, low_ref, w_ref, v_ref, out_ref, a_high, a_low):
    @pl.when(pl.program_id(0) == 0)
    def _():
        load_advance(w_ref, v_ref, a_high, a_low, scale)

    high, low = high_ref[...], low_ref[...]
    put_scores(
        out_ref, mul(high, a_high[...]) + mul(high, a_low[...]) + mul(low, a_high[...])
    )


def rescore(high, low, weights, velocity, scale):
    count, width = high.shape
    classes = weights.shape[1]
    block = 512
    whole = lambda shape: pl.BlockSpec(shape, lambda i: (0, 0), pipeline_mode=pl.Buffered(1))
    return pl.pallas_call(
        functools.partial(rescore_kernel, scale),
        grid=(count // block,),
        out_shape=jax.ShapeDtypeStruct((count // 128, CLASS_PAD, 128), jnp.float32),
        in_specs=[
            pl.BlockSpec((block, width), lambda i: (i, 0)),
            pl.BlockSpec((block, width), lambda i: (i, 0)),
            whole((width, classes)),
            whole((width, classes)),
        ],
        out_specs=pl.BlockSpec((block // 128, CLASS_PAD, 128), lambda i: (i, 0, 0)),
        scratch_shapes=[
            pltpu.VMEM((width, 256), jnp.bfloat16),
            pltpu.VMEM((width, 256), jnp.bfloat16),
        ],
        compiler_params=pltpu.CompilerParams(vmem_limit_bytes=VMEM_LIMIT),
        name="rescore",
    )(high, low, weights, velocity)


def gradient_kernel(scale, classes, scores_ref, labels_ref, high_ref, low_ref, out_ref, stack):
    groups = scores_ref.shape[0]
    step = pl.program_id(0)
    row = lax.broadcasted_iota(jnp.int32, (CLASS_PAD, 128), 0)
    for k in range(groups):
        scores = jnp.where(row < classes, scores_ref[k], -jnp.inf)
        exponent = jnp.exp(scores - jnp.max(scores, axis=0, keepdims=True))
        probability = exponent / jnp.sum(exponent, axis=0, keepdims=True)
        label = labels_ref[pl.ds(step * groups + k, 1), :]
        residual = (probability - jnp.where(row == label, 1.0, 0.0)) * scale
        at = pl.ds(128 * k, 128)
        stack[:CLASS_PAD, at], stack[CLASS_PAD:, at] = split(residual)
    both = mul(stack[...], high_ref[...])
    value = both[:CLASS_PAD] + both[CLASS_PAD:] + mul(stack[:CLASS_PAD, :], low_ref[...])

    @pl.when(step == 0)
    def _():
        out_ref[...] = value

    @pl.when(step > 0)
    def _():
        out_ref[...] += value


def make_gradient(scores, labels, high, low, scale, classes):
    count, width = high.shape
    block = 512
    groups = block // 128
    return pl.pallas_call(
        functools.partial(gradient_kernel, scale, classes),
        grid=(count // block,),
        out_shape=jax.ShapeDtypeStruct((CLASS_PAD, width), jnp.float32),
        in_specs=[
            pl.BlockSpec((groups, CLASS_PAD, 128), lambda i: (i, 0, 0)),
            pl.BlockSpec((count // 128, 128), lambda i: (0, 0), pipeline_mode=pl.Buffered(1)),
            pl.BlockSpec((block, width), lambda i: (i, 0)),
            pl.BlockSpec((block, width), lambda i: (i, 0)),
        ],
        out_specs=pl.BlockSpec((CLASS_PAD, width), lambda i: (0, 0)),
        scratch_shapes=[pltpu.VMEM((2 * CLASS_PAD, block), jnp.bfloat16)],
        compiler_params=pltpu.CompilerParams(vmem_limit_bytes=VMEM_LIMIT),
        name="make_gradient",
    )(scores, labels, high, low)


def update_kernel(
    count_all, g_ref, w_ref, v_ref, w_out, v_out, other, squares, others, send_sems, recv_sems
):
    pos = positions()
    partner = {"frame": 1 - lax.axis_index("frame")}
    greet(
        [partner]
        + [{"feat": feat_at(pos, dim, step)} for dim in "zxy" for step in (1, 2, 3)]
    )
    copies = Copies(send_sems, recv_sems)
    classes = w_ref.shape[1]
    width = g_ref.shape[1]
    copies.send(g_ref, other, partner).wait_recv()

    def square(j, total):
        at = pl.ds(pl.multiple_of(j * 128, 128), 128)
        value = g_ref[:, at] + other[:, at]
        value = value * value
        return total + jnp.sum(value.reshape(CLASS_PAD // 8, 8, 128), axis=0)

    squares[0] = lax.fori_loop(0, width // 128, square, jnp.zeros((8, 128), jnp.float32))
    for stage, dim in enumerate("zxy"):
        parts = [
            copies.send(
                squares.at[stage], others.at[stage, slot], {"feat": feat_at(pos, dim, step)}
            )
            for slot, step in enumerate((2, 1, 3))
        ]
        for copy in parts:
            copy.wait_recv()
        squares[stage + 1] = (squares[stage] + others[stage, 0]) + (
            others[stage, 1] + others[stage, 2]
        )
    square_sum = jnp.sum(squares[3], axis=(0, 1), keepdims=True)
    rate = STEP_RATE / jnp.sqrt(square_sum / count_all + EPSILON)

    def update(j, carry):
        at = pl.ds(pl.multiple_of(j * 128, 128), 128)
        flipped = (g_ref[:, at] + other[:, at]).T
        speed = MOMENTUM * v_ref[at, :] - rate * flipped[:, :classes]
        v_out[at, :] = speed
        w_out[at, :] = w_ref[at, :] + speed
        return carry

    lax.fori_loop(0, width // 128, update, 0)
    copies.wait_sends()


def update(gradient, weights, velocity, count_all, collective_id):
    f32 = jnp.float32
    shape = jax.ShapeDtypeStruct(weights.shape, f32)
    vmem = pl.BlockSpec(memory_space=pltpu.VMEM)
    return pl.pallas_call(
        functools.partial(update_kernel, count_all),
        out_shape=[shape, shape],
        in_specs=[vmem] * 3,
        out_specs=[vmem] * 2,
        scratch_shapes=[
            pltpu.VMEM(gradient.shape, f32),
            pltpu.VMEM((4, 8, 128), f32),
            pltpu.VMEM((3, 3, 8, 128), f32),
            pltpu.SemaphoreType.DMA((10,)),
            pltpu.SemaphoreType.DMA((10,)),
        ],
        compiler_params=pltpu.CompilerParams(
            collective_id=collective_id, has_side_effects=True, vmem_limit_bytes=VMEM_LIMIT
        ),
        name=f"update_{collective_id}",
    )(gradient, weights, velocity)


def on_device(frames, labels, proj, phase, class_weights, velocity):
    feat_count = 64 * proj.shape[1]
    classes = class_weights.shape[1]
    scale = math.sqrt(2.0 / feat_count)
    count_all = feat_count * classes
    count = labels.shape[0]
    labels = labels.reshape(count // 128, 128)
    everyone = gather_frames(frames).reshape(count, frames.shape[1])
    high, low, partial = make_features(everyone, proj, phase, class_weights, velocity, scale)
    units = (count // 64, UNIT, 128)
    for iteration in range(2):
        if iteration:
            partial = rescore(high, low, class_weights, velocity, scale)
        scores = sum_scores(partial.reshape(units), 1 + 2 * iteration).reshape(partial.shape)
        gradient = make_gradient(scores, labels, high, low, scale, classes)
        class_weights, velocity = update(
            gradient, class_weights, velocity, count_all, 2 + 2 * iteration
        )
    return class_weights, velocity


def solution(mesh):
    return jax.shard_map(
        on_device,
        mesh=mesh,
        in_specs=(
            P(("frame", "feat"), None),
            P("frame"),
            P(None, "feat"),
            P("feat"),
            P("feat", None),
            P("feat", None),
        ),
        out_specs=(P("feat", None), P("feat", None)),
        check_vma=False,
    )
```

time: 1260 us -> 282 us (0.22)
  matrix products: 468 us -> 0 us
  waiting for transfers between devices: 380 us -> 0 us
  blocking collectives: 359 us -> 0 us
  Pallas kernels: 0 us -> 272 us
  other arithmetic: 16.4 us -> 0 us
  between operations: 15.7 us -> 0.69 us
    dot_general x5 -> x0, matrix products: 468 us -> none  [the longest x2 224 us: on_device(): jnp.dot(features, advance, precision=lax.Precision.HIGHEST, preferred_ele...]
    psum x2 -> x0, blocking collectives: 359 us -> none  [on_device(): square_sum = lax.psum(jnp.sum(gradient * gradient), 'feat')]
    psum x4 -> x0, waiting for transfers between devices: 304 us -> none  [the longest x2 258 us: on_device(): scores = lax.psum(partial_value, 'feat')]
    pallas_call x0 -> x9, Pallas kernels: none -> 272 us  [the longest x2 82.6 us: sum_scores(): pl.pallas_call(scores_kernel, out_shape=jax.ShapeDtypeStruct(partial_scor...]
    all_gather x1 -> x0, waiting for transfers between devices: 75.3 us -> none  [on_device(): lax.all_gather(frames, 'feat', axis=0, tiled=True)]
  transfers between devices with their start and end apart: 5 -> 0, of which waited for: 5 -> 0; matrix products, arithmetic and copies ran while one was open for 0% -> 0% of each run, Pallas kernels for 0% -> 0%
where the time goes in v1:
time: 282 us; the launch traced here: 281 us
  Pallas kernels  272 us (96%)
  local copies, waits for them, and re-layouts  9.1 us (3%)
    pallas_call x2, Pallas kernels, sum_scores(): pl.pallas_call(scores_kernel, out_shape=jax.ShapeDtypeStruct(partial_scor...  82.6 us
    pallas_call x1, Pallas kernels, make_features(): pl.pallas_call(functools.partial(features_kernel, scale), grid=(count //...  62.2 us
    pallas_call x2, Pallas kernels, update(): pl.pallas_call(functools.partial(update_kernel, count_all), out_shape=[sh...  40.6 us
    pallas_call x1, Pallas kernels, gather_frames(): pl.pallas_call(frames_kernel, out_shape=jax.ShapeDtypeStruct((4, 4, 4, ro...  40.3 us
    pallas_call x2, Pallas kernels, make_gradient(): pl.pallas_call(functools.partial(gradient_kernel, scale, classes), grid=(...  28.6 us
    pallas_call x1, Pallas kernels, rescore(): pl.pallas_call(functools.partial(rescore_kernel, scale), grid=(count // b...  17.3 us

profile of v1, /device:TPU:0, one launch (start us, length us, event | category | flops | bytes accessed | tf_op | source)
XLA Modules:
  0.0 281.4 jit_solution(14266765890699082694)
XLA Ops:
  0.6 0.0 copy-start.1
  0.6 2.9 %copy.8.w_ref = f32[2048,147]{1,0:T(8,128)} copy(f32[2048,147]{0,1:T(8,128)} %param.10) | data formatting | bytes 2408448 | tf_op args[4]
  3.5 0.0 copy-done.1
  3.5 1.8 copy.9.v_ref
  5.3 40.3 %gather_frames.1 = f32[4,4,4,48,440]{4,3,2,1,0:T(8,128)} custom-call(f32[48,440]{1,0:T(8,128)} %x_ref.1), custom_call_target="tpu_custom_call" | custom-call | tf_op jit(solution)/shard_map/gather_frames/pallas_call | solution.py:146
  45.6 62.2 %make_features.1 = (bf16[3072,2048]{1,0:T(8,128)(2,1)}, bf16[3072,2048]{1,0:T(8,128)(2,1)}, f32[24,160,128]{2,1,0:T(8,128)}) custom-call(f32[3072,440]{1,0:T(8,128)} %bitcast.7, f32[440,2048]{1,0:T(8,128)} %proj_ref.1, f32[1,2048]{1,0:T(1,128)} %bitcast.14, f32[2048,147]{1,0:T(8,128)} %copy.8.w_ref, f32[2048,147]{1,0:T(8,128)} %copy.9.v_ref), custom_call_target="tpu_custom_call" | custom-call | tf_op jit(solution)/shard_map/make_features/pallas_call | solution.py:366
  107.7 41.3 %sum_scores_1.1 = f32[48,80,128]{2,1,0:T(8,128)} custom-call(f32[48,80,128]{2,1,0:T(8,128)} %bitcast.11), custom_call_target="tpu_custom_call" | custom-call | tf_op jit(solution)/shard_map/sum_scores_1/pallas_call | solution.py:251
  149.0 14.3 %make_gradient.2.g_ref = f32[160,2048]{1,0:T(8,128)} custom-call(f32[24,160,128]{2,1,0:T(8,128)} %bitcast.9, s32[24,128]{1,0:T(8,128)} %bitcast.12, bf16[3072,2048]{1,0:T(8,128)(2,1)} %get-tuple-element.7.high_ref, bf16[3072,2048]{1,0:T(8,128)(2,1)} %get-tuple-element.8.low_ref), custom_call_target="tpu_custom_call" | custom-call | tf_op jit(solution)/shard_map/make_gradient/pallas_call | solution.py:463
  163.3 20.4 %update_2.1 = (f32[2048,147]{1,0:T(8,128)}, f32[2048,147]{1,0:T(8,128)}) custom-call(f32[160,2048]{1,0:T(8,128)} %make_gradient.2.g_ref, f32[2048,147]{1,0:T(8,128)} %copy.8.w_ref, f32[2048,147]{1,0:T(8,128)} %copy.9.v_ref), custom_call_target="tpu_custom_call" | custom-call | tf_op jit(solution)/shard_map/update_2/pallas_call | solution.py:532
  183.7 17.3 %rescore.1 = f32[24,160,128]{2,1,0:T(8,128)} custom-call(bf16[3072,2048]{1,0:T(8,128)(2,1)} %get-tuple-element.7.high_ref, bf16[3072,2048]{1,0:T(8,128)(2,1)} %get-tuple-element.8.low_ref, f32[2048,147]{1,0:T(8,128)} %get-tuple-element.10.w_ref, f32[2048,147]{1,0:T(8,128)} %get-tuple-element.11.v_ref), custom_call_target="tpu_custom_call" | custom-call | tf_op jit(solution)/shard_map/rescore/pallas_call | solution.py:415
  201.0 41.4 %sum_scores_3.1 = f32[48,80,128]{2,1,0:T(8,128)} custom-call(f32[48,80,128]{2,1,0:T(8,128)} %bitcast.10), custom_call_target="tpu_custom_call" | custom-call | tf_op jit(solution)/shard_map/sum_scores_3/pallas_call | solution.py:251
  242.4 14.3 %make_gradient.3.g_ref = f32[160,2048]{1,0:T(8,128)} custom-call(f32[24,160,128]{2,1,0:T(8,128)} %bitcast.8, s32[24,128]{1,0:T(8,128)} %bitcast.13, bf16[3072,2048]{1,0:T(8,128)(2,1)} %get-tuple-element.7.high_ref, bf16[3072,2048]{1,0:T(8,128)(2,1)} %get-tuple-element.8.low_ref), custom_call_target="tpu_custom_call" | custom-call | tf_op jit(solution)/shard_map/make_gradient/pallas_call | solution.py:463
  256.7 20.2 %update_4.1 = (f32[2048,147]{1,0:T(8,128)}, f32[2048,147]{1,0:T(8,128)}) custom-call(f32[160,2048]{1,0:T(8,128)} %make_gradient.3.g_ref, f32[2048,147]{1,0:T(8,128)} %get-tuple-element.10.w_ref, f32[2048,147]{1,0:T(8,128)} %get-tuple-element.11.v_ref), custom_call_target="tpu_custom_call" | custom-call | tf_op jit(solution)/shard_map/update_4/pallas_call | solution.py:532
  276.9 0.0 copy-start
  276.9 2.8 %copy.12 = f32[2048,147]{0,1:T(8,128)} copy(f32[2048,147]{1,0:T(8,128)} %get-tuple-element.12) | data formatting | bytes 2408448 | tf_op jit(solution)/shard_map/update_4/pallas_call | solution.py:532
  279.8 0.0 copy-done
  279.8 1.6 copy.13
Async XLA Ops:
  0.6 2.9 %copy-start.1 = (f32[2048,147]{0,1:T(8,128)S(1)}, f32[2048,147]{0,1:T(8,128)}, u32[]{:S(2)}) copy-start(f32[2048,147]{0,1:T(8,128)} %param.11) | copy-start | bytes 3612676
  276.9 2.8 %copy-start = (f32[2048,147]{1,0:T(8,128)S(1)}, f32[2048,147]{1,0:T(8,128)}, u32[]{:S(2)}) copy-start(f32[2048,147]{1,0:T(8,128)} %get-tuple-element.13) | copy-start | bytes 3612676

commit v2 on v0

v2 whole, which is shorter than its diff:
```python
import functools
import math

import jax
import jax.numpy as jnp
from jax import lax
from jax.experimental import pallas as pl
from jax.experimental.pallas import tpu as pltpu
from jax.sharding import PartitionSpec as P

MOMENTUM = 0.9
STEP_RATE = 0.05
EPSILON = 1e-06
ITERS = 2
TURN = 1.0 / (2.0 * math.pi)
ROUNDER = 1.5 * 2.0**23
SINE = (
    6.283185160089458,
    -41.34165503141172,
    81.60100407300267,
    -76.54978228814288,
    39.53670602749812,
)
MESH = pl.DeviceIdType.MESH
VMEM_LIMIT = 67043328
CLASS_PAD = 160
UNIT = 40
COLOURS = (("y", "x", "z"), ("x", "z", "y"), ("z", "y", "x"))
FRAME_COPIES = 3 * 3 * 6
CHUNKS = 2
SCORE_COPIES = CHUNKS * 3 * (3 + 3 + 3 + 3 + 6)
SQUARE_COPIES = 9
TILE = 512


def positions():
    index = lax.axis_index("feat")
    return {"z": index // 16, "x": (index // 4) % 4, "y": index % 4}


class Copies:
    def __init__(self, pos, send_sems, recv_sems, first):
        self.pos, self.send_sems, self.recv_sems = pos, send_sems, recv_sems
        self.first, self.made = first, []

    def device(self, dim, step):
        moved = dict(self.pos)
        moved[dim] = (self.pos[dim] + step) % 4
        return {"feat": moved["z"] * 16 + moved["x"] * 4 + moved["y"]}

    def make(self, src, dst, dim, step):
        slot = self.first + len(self.made)
        copy = pltpu.make_async_remote_copy(
            src_ref=src,
            dst_ref=dst,
            send_sem=self.send_sems.at[slot],
            recv_sem=self.recv_sems.at[slot],
            device_id=self.device(dim, step),
            device_id_type=MESH,
        )
        self.made.append(copy)
        return copy

    def send(self, src, dst, dim, step):
        copy = self.make(src, dst, dim, step)
        copy.start()
        return copy

    def wait_sends(self):
        for copy in self.made:
            copy.wait_send()


def ring_copies(copies, dim, source, block):
    here = copies.pos[dim]
    before, after = (here + 3) % 4, (here + 1) % 4
    return (
        copies.make(source(0), block(here, 0), dim, 1),
        copies.make(source(1), block(here, 1), dim, 3),
        copies.make(source(1), block(here, 1), dim, 1),
        copies.make(source(0), block(here, 0), dim, 3),
        copies.make(block(before, 0), block(before, 0), dim, 1),
        copies.make(block(after, 1), block(after, 1), dim, 3),
    )


def gather_ring(copies, dim, source, block):
    ring = ring_copies(copies, dim, source, block)
    for copy in ring[:4]:
        copy.start()
    yield
    ring[0].wait_recv()
    ring[4].start()
    ring[1].wait_recv()
    ring[5].start()
    yield
    for copy in ring[2:]:
        copy.wait_recv()


def advance_all(streams):
    alive = []
    for stream in streams:
        try:
            next(stream)
            alive.append(stream)
        except StopIteration:
            pass
    return alive


def split(value):
    high = value.astype(jnp.bfloat16)
    return high, (value - high.astype(jnp.float32)).astype(jnp.bfloat16)


def mul(left, right):
    return jnp.dot(left, right, preferred_element_type=jnp.float32)


def mul_flipped(left, right):
    return lax.dot_general(
        left, right, (((1,), (1,)), ((), ())), preferred_element_type=jnp.float32
    )


def sum_chunk(copies, chunk, colour, p_ref, total, wide, kept, narrow, unit, others):
    d1, d2, d3 = COLOURS[colour]
    pos = copies.pos
    a, b = pos[d1], pos[d2]
    base = 48 * chunk + 16 * colour
    c = 3 * chunk + colour
    steps = (2, 1, 3)

    def row(i):
        return pl.ds(base + 4 * i, 4)

    sent = [
        copies.send(p_ref.at[row((a + step) % 4)], wide.at[c, slot], d1, step)
        for slot, step in enumerate(steps)
    ]
    yield
    for copy in sent:
        copy.wait_recv()
    kept[c] = (p_ref[row(a)] + wide[c, 0]) + (wide[c, 1] + wide[c, 2])
    sent = [
        copies.send(kept.at[c, (b + step) % 4], narrow.at[c, slot], d2, step)
        for slot, step in enumerate(steps)
    ]
    yield
    for copy in sent:
        copy.wait_recv()
    unit[c] = (kept[c, b] + narrow[c, 0]) + (narrow[c, 1] + narrow[c, 2])
    sent = [
        copies.send(unit.at[c], others.at[c, slot], d3, step) for slot, step in enumerate(steps)
    ]
    yield
    for copy in sent:
        copy.wait_recv()
    mine = base + 4 * a + b
    total[mine] = (unit[c] + others[c, 0]) + (others[c, 1] + others[c, 2])
    sent = [copies.send(total.at[mine], total.at[mine], d2, step) for step in steps]
    yield
    for copy in sent:
        copy.wait_recv()

    def block(q, h):
        return total.at[pl.ds(base + 4 * q + 2 * h, 2)]

    yield from gather_ring(copies, d1, lambda h: block(a, h), block)


def kernel(
    scale, count_all, x_hbm, labels_ref, proj_hbm, phase_ref, w_hbm, v_hbm, w_ref, v_ref,
    everyone, proj_ref, p_high, p_low, x_pad, f_high, f_low, a_stack, p_ref, total,
    wide, kept, narrow, unit, others, r_stack, g_ref, g_other, squares, square_parts,
    send_sems, recv_sems, pair_send, pair_recv, load_sems,
):
    pos = positions()
    classes, width = w_ref.shape
    depth = x_hbm.shape[1]
    frames = f_high.shape[0]
    partner = {"frame": 1 - lax.axis_index("frame")}
    own_x = pltpu.make_async_copy(
        x_hbm, everyone.at[pos["z"], pos["x"], pos["y"]], load_sems.at[0]
    )
    load_proj = pltpu.make_async_copy(proj_hbm, proj_ref, load_sems.at[1])
    load_w = pltpu.make_async_copy(w_hbm, w_ref, load_sems.at[2])
    load_v = pltpu.make_async_copy(v_hbm, v_ref, load_sems.at[3])
    for load in (own_x, load_proj, load_w, load_v):
        load.start()

    copies = Copies(pos, send_sems, recv_sems, 0)
    barrier = pltpu.get_barrier_semaphore()
    peers = [partner] + [copies.device(dim, step) for dim in "zxy" for step in (1, 2, 3)]
    for peer in peers:
        pl.semaphore_signal(barrier, inc=1, device_id=peer, device_id_type=MESH)
    pl.semaphore_wait(barrier, len(peers))

    def piece(dims, colour, done, q, h):
        at = tuple(
            slice(None) if name in done else (q if name == dims[len(done)] else pos[name])
            for name in "zxy"
        )
        return everyone.at[at + (pl.ds(16 * colour + 8 * h, 8),)]

    def near(colour):
        dims = COLOURS[colour]
        for count in range(2):
            block = functools.partial(piece, dims, colour, dims[:count])
            if count == 0:
                source = lambda h: x_hbm.at[pl.ds(16 * colour + 8 * h, 8)]
            else:
                source = functools.partial(block, pos[dims[1]])
            yield from gather_ring(copies, dims[count], source, block)
            if count == 0 and colour == 0:
                own_x.wait()

    def prepare_proj():
        load_proj.wait()
        whole = depth // 16 * 16
        step = 48
        for k in range(whole // step):
            at = pl.ds(k * step, step)
            p_high[at, :], p_low[at, :] = split(proj_ref[at, :] * TURN)
        phase = phase_ref[...] * TURN
        top = phase.astype(jnp.bfloat16).astype(jnp.float32)
        row = lax.broadcasted_iota(jnp.int32, (8, width), 0)
        tail = jnp.where(row == 0, top, jnp.where(row == 1, phase - top, 0.0))
        last = jnp.concatenate([proj_ref[whole:depth, :] * TURN, tail], axis=0)
        p_high[whole : whole + 16, :], p_low[whole : whole + 16, :] = split(last)
        rest = p_high.shape[0] - whole - 16
        p_high[whole + 16 :, :] = jnp.zeros((rest, width), jnp.bfloat16)
        p_low[whole + 16 :, :] = jnp.zeros((rest, width), jnp.bfloat16)

    def prepare_rest():
        lane = lax.broadcasted_iota(jnp.int32, x_pad.shape, 1)
        x_pad[...] = jnp.where((lane == depth) | (lane == depth + 1), 1.0, 0.0)
        a_stack[...] = jnp.zeros_like(a_stack)
        load_w.wait()
        load_v.wait()

    streams = advance_all([near(colour) for colour in range(3)])
    prepare_proj()
    streams = advance_all(streams)
    prepare_rest()
    while streams:
        streams = advance_all(streams)

    far = []
    for colour, dims in enumerate(COLOURS):
        block = functools.partial(piece, dims, colour, dims[:2])
        far.append(ring_copies(copies, dims[2], functools.partial(block, pos[dims[2]]), block))
    for slot in range(4):
        for ring in far:
            ring[slot].start()

    def features(i, carry):
        def when_arrived(step, slots):
            @pl.when(i == step)
            def _():
                for slot in slots:
                    for ring in far:
                        ring[slot].wait_recv()
                        if slot < 2:
                            ring[slot + 4].start()

        when_arrived(1, (0, 1))
        for slot in range(2, 6):
            when_arrived(slot + 2, (slot,))
        h = jnp.where((i == 1) | (i == 3) | (i == 4) | (i == 7), 1, 0)
        off = jnp.where(i < 2, 0, jnp.where(i > 5, 2, jnp.where((i == 2) | (i == 4), 3, 1)))
        rows = []
        for colour, dims in enumerate(COLOURS):
            q = (pos[dims[2]] + off) % 4
            at = tuple(q if name == dims[2] else slice(None) for name in "zxy")
            lines = pl.ds(pl.multiple_of(16 * colour + 8 * h, 8), 8)
            part = everyone[at + (lines, slice(None))]
            x_pad[128 * colour : 128 * (colour + 1), :depth] = part.reshape(128, depth)
            rows.append(pl.ds(pl.multiple_of(128 * (8 * colour + 4 * h + q), 128), 128))
        count = x_pad.shape[0]
        high, low = split(x_pad[...])
        both = jnp.concatenate([high, low], axis=0)
        step = 256
        for n in range(width // step):
            at = pl.ds(n * step, step)
            turns = mul(both, p_high[:, at])
            turns = turns[:count] + turns[count:] + mul(high, p_low[:, at])
            turns = turns - ((turns + ROUNDER) - ROUNDER)
            quarter = 0.25 - jnp.abs(turns)
            square = quarter * quarter
            value = SINE[4]
            for coefficient in SINE[3::-1]:
                value = value * square + coefficient
            top, bottom = split(value * quarter)
            for colour in range(3):
                f_high[rows[colour], at] = top[128 * colour : 128 * (colour + 1)]
                f_low[rows[colour], at] = bottom[128 * colour : 128 * (colour + 1)]
        return carry

    lax.fori_loop(0, 8, features, 0)
    copies.wait_sends()

    def exchange(iteration, n):
        return pltpu.make_async_remote_copy(
            src_ref=g_ref.at[n],
            dst_ref=g_other.at[iteration, n],
            send_sem=pair_send.at[n],
            recv_sem=pair_recv.at[iteration, n],
            device_id=partner,
            device_id_type=MESH,
        )

    tiles = width // TILE

    def optimize(iteration, carry):
        copies = Copies(pos, send_sems, recv_sems, FRAME_COPIES)

        def look_ahead(n, carry):
            at = pl.ds(pl.multiple_of(n * TILE, TILE), TILE)
            high, low = split((w_ref[:, at] + MOMENTUM * v_ref[:, at]) * scale)
            a_stack[:classes, at] = high
            a_stack[CLASS_PAD : CLASS_PAD + classes, at] = low
            return carry

        lax.fori_loop(0, tiles, look_ahead, 0)

        def score(n, carry):
            at = pl.ds(pl.multiple_of(n * TILE, TILE), TILE)
            both = mul_flipped(a_stack[...], f_high[at, :])
            low = mul_flipped(a_stack[:CLASS_PAD, :], f_low[at, :])
            scores = both[:CLASS_PAD] + both[CLASS_PAD:] + low
            for k in range(TILE // 128):
                part = scores[:, 128 * k : 128 * (k + 1)].reshape(4, UNIT, 128)
                p_ref[pl.ds(4 * (n * (TILE // 128) + k), 4)] = part
            return carry

        def residuals(block, carry):
            row = lax.broadcasted_iota(jnp.int32, (CLASS_PAD, 128), 0)
            scores = total[pl.ds(4 * block, 4)].reshape(CLASS_PAD, 128)
            scores = jnp.where(row < classes, scores, -jnp.inf)
            exponent = jnp.exp(scores - jnp.max(scores, axis=0, keepdims=True))
            probability = exponent / jnp.sum(exponent, axis=0, keepdims=True)
            label = labels_ref[pl.ds(block, 1), :]
            residual = (probability - jnp.where(row == label, 1.0, 0.0)) * scale
            at = pl.ds(pl.multiple_of(block * 128, 128), 128)
            r_stack[:CLASS_PAD, at], r_stack[CLASS_PAD:, at] = split(residual)
            return carry

        def gradient(chunk, n, carry):
            at = pl.ds(pl.multiple_of(n * TILE, TILE), TILE)
            rows = pl.ds(chunk * (frames // CHUNKS), frames // CHUNKS)
            both = mul(r_stack[:, rows], f_high[rows, at])
            value = both[:CLASS_PAD] + both[CLASS_PAD:]
            value = value + mul(r_stack[:CLASS_PAD, rows], f_low[rows, at])
            if chunk == 0:
                g_ref[n] = value
            else:
                g_ref[n] = g_ref[n] + value
            if chunk == CHUNKS - 1:
                exchange(iteration, n).start()
            return carry

        def streams(chunk):
            return [
                sum_chunk(
                    copies, chunk, colour, p_ref, total, wide, kept, narrow, unit, others
                )
                for colour in range(3)
            ]

        per_chunk = frames // TILE // CHUNKS
        lax.fori_loop(0, per_chunk, score, 0)
        early = advance_all(streams(0))
        lax.fori_loop(per_chunk, 2 * per_chunk, score, 0)
        late = advance_all(streams(1))
        while early:
            early = advance_all(early)
            if early:
                late = advance_all(late)
        blocks = frames // 128 // CHUNKS
        lax.fori_loop(0, blocks, residuals, 0)
        late = advance_all(late)
        lax.fori_loop(0, tiles, functools.partial(gradient, 0), 0)
        while late:
            late = advance_all(late)
        lax.fori_loop(blocks, 2 * blocks, residuals, 0)
        lax.fori_loop(0, tiles, functools.partial(gradient, 1), 0)

        summed = jnp.zeros((8, TILE), jnp.float32)
        for n in range(tiles):
            exchange(iteration, n).wait_recv()
            value = g_ref[n] + g_other[iteration, n]
            value = value * value
            summed = summed + jnp.sum(value.reshape(CLASS_PAD // 8, 8, TILE), axis=0)
        squares[0] = jnp.sum(
            jnp.stack([summed[:, 128 * k : 128 * (k + 1)] for k in range(TILE // 128)]), axis=0
        )
        for stage, dim in enumerate("zxy"):
            sent = [
                copies.send(squares.at[stage], square_parts.at[stage, slot], dim, step)
                for slot, step in enumerate((2, 1, 3))
            ]
            for copy in sent:
                copy.wait_recv()
            squares[stage + 1] = (squares[stage] + square_parts[stage, 0]) + (
                square_parts[stage, 1] + square_parts[stage, 2]
            )
        square_sum = jnp.sum(squares[3], axis=(0, 1), keepdims=True)
        rate = STEP_RATE / jnp.sqrt(square_sum / count_all + EPSILON)

        def update(n, carry):
            at = pl.ds(pl.multiple_of(n * TILE, TILE), TILE)
            value = g_ref[n, :classes] + g_other[iteration, n, :classes]
            speed = MOMENTUM * v_ref[:, at] - rate * value
            v_ref[:, at] = speed
            w_ref[:, at] = w_ref[:, at] + speed
            return carry

        lax.fori_loop(0, tiles, update, 0)
        copies.wait_sends()
        for n in range(tiles):
            exchange(iteration, n).wait_send()
        return carry

    lax.fori_loop(0, ITERS, optimize, 0)


def regroup(labels):
    parts = labels.reshape(4, 4, 4, 3, 2, 8)
    orders = ((3, 0, 1, 2, 4), (3, 2, 0, 1, 4), (3, 1, 0, 2, 4))
    return jnp.concatenate(
        [parts[:, :, :, c].transpose(order).reshape(8, 128) for c, order in enumerate(orders)]
    )


def on_device(frames, labels, proj, phase, class_weights, velocity):
    depth, width = proj.shape
    classes = class_weights.shape[1]
    feat_count = 64 * width
    scale = math.sqrt(2.0 / feat_count)
    count = labels.shape[0]
    f32, bf16 = jnp.float32, jnp.bfloat16
    units = count // 128 * 4
    colours = 3 * CHUNKS
    anywhere = pl.BlockSpec(memory_space=pl.ANY)
    vmem = pl.BlockSpec(memory_space=pltpu.VMEM)
    shape = jax.ShapeDtypeStruct((classes, width), f32)
    weights, speed = pl.pallas_call(
        functools.partial(kernel, scale, feat_count * classes),
        out_shape=[shape, shape],
        in_specs=[anywhere, vmem, anywhere, vmem, anywhere, anywhere],
        out_specs=[vmem, vmem],
        scratch_shapes=[
            pltpu.VMEM((4, 4, 4) + frames.shape, f32),
            pltpu.VMEM((depth, width), f32),
            pltpu.VMEM((512, width), bf16),
            pltpu.VMEM((512, width), bf16),
            pltpu.VMEM((384, 512), f32),
            pltpu.VMEM((count, width), bf16),
            pltpu.VMEM((count, width), bf16),
            pltpu.VMEM((2 * CLASS_PAD, width), bf16),
            pltpu.VMEM((units, UNIT, 128), f32),
            pltpu.VMEM((units, UNIT, 128), f32),
            pltpu.VMEM((colours, 3, 4, UNIT, 128), f32),
            pltpu.VMEM((colours, 4, UNIT, 128), f32),
            pltpu.VMEM((colours, 3, UNIT, 128), f32),
            pltpu.VMEM((colours, UNIT, 128), f32),
            pltpu.VMEM((colours, 3, UNIT, 128), f32),
            pltpu.VMEM((2 * CLASS_PAD, count), bf16),
            pltpu.VMEM((width // TILE, CLASS_PAD, TILE), f32),
            pltpu.VMEM((ITERS, width // TILE, CLASS_PAD, TILE), f32),
            pltpu.VMEM((4, 8, 128), f32),
            pltpu.VMEM((3, 3, 8, 128), f32),
            pltpu.SemaphoreType.DMA((FRAME_COPIES + SCORE_COPIES + SQUARE_COPIES,)),
            pltpu.SemaphoreType.DMA((FRAME_COPIES + SCORE_COPIES + SQUARE_COPIES,)),
            pltpu.SemaphoreType.DMA((width // TILE,)),
            pltpu.SemaphoreType.DMA((ITERS, width // TILE)),
            pltpu.SemaphoreType.DMA((4,)),
        ],
        compiler_params=pltpu.CompilerParams(
            collective_id=0, has_side_effects=True, vmem_limit_bytes=VMEM_LIMIT
        ),
        name="optimize",
    )(frames, regroup(labels), proj, phase.reshape(1, width), class_weights.T, velocity.T)
    return weights.T, speed.T


def solution(mesh):
    return jax.shard_map(
        on_device,
        mesh=mesh,
        in_specs=(
            P(("frame", "feat"), None),
            P("frame"),
            P(None, "feat"),
            P("feat"),
            P("feat", None),
            P("feat", None),
        ),
        out_specs=(P("feat", None), P("feat", None)),
        check_vma=False,
    )
```

time: 1260 us -> 179 us (0.14)
  matrix products: 468 us -> 0 us
  waiting for transfers between devices: 380 us -> 0 us
  blocking collectives: 359 us -> 0 us
  Pallas kernels: 0 us -> 172 us
  other arithmetic: 16.4 us -> 0.61 us
  between operations: 15.7 us -> 0.69 us
    dot_general x5 -> x0, matrix products: 468 us -> none  [the longest x2 224 us: on_device(): jnp.dot(features, advance, precision=lax.Precision.HIGHEST, preferred_ele...]
    psum x2 -> x0, blocking collectives: 359 us -> none  [on_device(): square_sum = lax.psum(jnp.sum(gradient * gradient), 'feat')]
    psum x4 -> x0, waiting for transfers between devices: 304 us -> none  [the longest x2 258 us: on_device(): scores = lax.psum(partial_value, 'feat')]
    pallas_call x0 -> x1, Pallas kernels: none -> 172 us  [on_device(): pl.pallas_call(functools.partial(kernel, scale, feat_count * classes), ou...]
    all_gather x1 -> x0, waiting for transfers between devices: 75.3 us -> none  [on_device(): lax.all_gather(frames, 'feat', axis=0, tiled=True)]
  transfers between devices with their start and end apart: 5 -> 0, of which waited for: 5 -> 0; matrix products, arithmetic and copies ran while one was open for 0% -> 0% of each run, Pallas kernels for 0% -> 0%
where the time goes in v2:
time: 179 us
  Pallas kernels  172 us (96%)
  local copies, waits for them, and re-layouts  5.04 us (3%)
    pallas_call x1, Pallas kernels, on_device(): pl.pallas_call(functools.partial(kernel, scale, feat_count * classes), ou...  172 us

profile of v2, /device:TPU:0, one launch (start us, length us, event | category | flops | bytes accessed | tf_op | source)
XLA Modules:
  0.0 178.8 jit_solution(3998448837082963664)
XLA Ops:
  0.6 1.0 reshape.19
  1.7 0.1 slice_bitcast_fusion.2
  1.8 0.1 reshape.20
  1.9 0.1 reshape.22
  2.0 0.1 reshape.21
  2.1 0.6 pad_add_fusion.labels_ref
  2.7 172.4 %optimize.1 = (f32[147,2048]{1,0:T(8,128)}, f32[147,2048]{1,0:T(8,128)}) custom-call(f32[48,440]{1,0:T(8,128)} %x_hbm.1, s32[24,128]{1,0:T(8,128)} %pad_add_fusion.labels_ref, f32[440,2048]{1,0:T(8,128)} %proj_hbm.1, f32[1,2048]{1,0:T(1,128)} %bitcast.21, f32[147,2048]{1,0:T(8,128)} %bitcast.17, f32[147,2048]{1,0:T(8,128)} %bitcast.18), custom_call_target="tpu_custom_call" | custom-call | tf_op jit(solution)/shard_map/optimize/pallas_call | solution.py:449
  175.2 0.0 copy-start
  175.2 2.5 %copy.15 = f32[2048,147]{0,1:T(8,128)} copy(f32[2048,147]{0,1:T(8,128)} %bitcast.20) | data formatting | bytes 2408448
  177.7 0.0 copy-done
  177.7 1.0 copy.16
  (3 shorter events, 0.1 us)
Async XLA Ops:
  175.2 2.6 %copy-start = (f32[147,2048]{1,0:T(8,128)S(1)}, f32[147,2048]{1,0:T(8,128)}, u32[]{:S(2)}) copy-start(f32[147,2048]{1,0:T(8,128)} %get-tuple-element.5) | copy-start | bytes 3612676

commit v3 on v2

--- a/solution.py
+++ b/solution.py
@@ -26,7 +26,7 @@
 CLASS_PAD = 160
 UNIT = 40
 COLOURS = (("y", "x", "z"), ("x", "z", "y"), ("z", "y", "x"))
-FRAME_COPIES = 3 * 3 * 6
+FRAME_COPIES = 3 * (3 + 6 + 6)
 CHUNKS = 2
 SCORE_COPIES = CHUNKS * 3 * (3 + 3 + 3 + 3 + 6)
 SQUARE_COPIES = 9
@@ -41,7 +41,7 @@
 class Copies:
     def __init__(self, pos, send_sems, recv_sems, first):
         self.pos, self.send_sems, self.recv_sems = pos, send_sems, recv_sems
-        self.first, self.made = first, []
+        self.slot, self.made = first, []
 
     def device(self, dim, step):
         moved = dict(self.pos)
@@ -49,7 +49,8 @@
         return {"feat": moved["z"] * 16 + moved["x"] * 4 + moved["y"]}
 
     def make(self, src, dst, dim, step):
-        slot = self.first + len(self.made)
+        slot = self.slot
+        self.slot += 1
         copy = pltpu.make_async_remote_copy(
             src_ref=src,
             dst_ref=dst,
@@ -69,6 +70,7 @@
     def wait_sends(self):
         for copy in self.made:
             copy.wait_send()
+        self.made = []
 
 
 def ring_copies(copies, dim, source, block):
@@ -172,7 +174,7 @@
 
 def kernel(
     scale, count_all, x_hbm, labels_ref, proj_hbm, phase_ref, w_hbm, v_hbm, w_ref, v_ref,
-    everyone, proj_ref, p_high, p_low, x_pad, f_high, f_low, a_stack, p_ref, total,
+    x_ref, everyone, proj_ref, p_high, p_low, f_high, f_low, a_stack, p_ref, p_next, total,
     wide, kept, narrow, unit, others, r_stack, g_ref, g_other, squares, square_parts,
     send_sems, recv_sems, pair_send, pair_recv, load_sems,
 ):
@@ -181,13 +183,11 @@
     depth = x_hbm.shape[1]
     frames = f_high.shape[0]
     partner = {"frame": 1 - lax.axis_index("frame")}
-    own_x = pltpu.make_async_copy(
-        x_hbm, everyone.at[pos["z"], pos["x"], pos["y"]], load_sems.at[0]
-    )
+    load_x = pltpu.make_async_copy(x_hbm, x_ref, load_sems.at[0])
     load_proj = pltpu.make_async_copy(proj_hbm, proj_ref, load_sems.at[1])
     load_w = pltpu.make_async_copy(w_hbm, w_ref, load_sems.at[2])
     load_v = pltpu.make_async_copy(v_hbm, v_ref, load_sems.at[3])
-    for load in (own_x, load_proj, load_w, load_v):
+    for load in (load_x, load_proj, load_w, load_v):
         load.start()
 
     copies = Copies(pos, send_sems, recv_sems, 0)
@@ -195,6 +195,11 @@
     peers = [partner] + [copies.device(dim, step) for dim in "zxy" for step in (1, 2, 3)]
     for peer in peers:
         pl.semaphore_signal(barrier, inc=1, device_id=peer, device_id_type=MESH)
+    load_x.wait()
+    lane = lax.broadcasted_iota(jnp.int32, (x_ref.shape[0], everyone.shape[4]), 1)
+    here = (pos["z"], pos["x"], pos["y"])
+    everyone[here] = jnp.where((lane == depth) | (lane == depth + 1), 1.0, 0.0)
+    everyone[here + (slice(None), pl.ds(0, depth))] = x_ref[...]
     pl.semaphore_wait(barrier, len(peers))
 
     def piece(dims, colour, done, q, h):
@@ -206,15 +211,13 @@
 
     def near(colour):
         dims = COLOURS[colour]
-        for count in range(2):
-            block = functools.partial(piece, dims, colour, dims[:count])
-            if count == 0:
-                source = lambda h: x_hbm.at[pl.ds(16 * colour + 8 * h, 8)]
-            else:
-                source = functools.partial(block, pos[dims[1]])
-            yield from gather_ring(copies, dims[count], source, block)
-            if count == 0 and colour == 0:
-                own_x.wait()
+        mine = everyone.at[here + (pl.ds(16 * colour, 16),)]
+        sent = [copies.send(mine, mine, dims[0], step) for step in (2, 1, 3)]
+        yield
+        for copy in sent:
+            copy.wait_recv()
+        block = functools.partial(piece, dims, colour, dims[:1])
+        yield from gather_ring(copies, dims[1], functools.partial(block, pos[dims[1]]), block)
 
     def prepare_proj():
         load_proj.wait()
@@ -234,8 +237,6 @@
         p_low[whole + 16 :, :] = jnp.zeros((rest, width), jnp.bfloat16)
 
     def prepare_rest():
-        lane = lax.broadcasted_iota(jnp.int32, x_pad.shape, 1)
-        x_pad[...] = jnp.where((lane == depth) | (lane == depth + 1), 1.0, 0.0)
         a_stack[...] = jnp.zeros_like(a_stack)
         load_w.wait()
         load_v.wait()
@@ -270,16 +271,15 @@
             when_arrived(slot + 2, (slot,))
         h = jnp.where((i == 1) | (i == 3) | (i == 4) | (i == 7), 1, 0)
         off = jnp.where(i < 2, 0, jnp.where(i > 5, 2, jnp.where((i == 2) | (i == 4), 3, 1)))
-        rows = []
+        rows, parts = [], []
         for colour, dims in enumerate(COLOURS):
             q = (pos[dims[2]] + off) % 4
             at = tuple(q if name == dims[2] else slice(None) for name in "zxy")
             lines = pl.ds(pl.multiple_of(16 * colour + 8 * h, 8), 8)
-            part = everyone[at + (lines, slice(None))]
-            x_pad[128 * colour : 128 * (colour + 1), :depth] = part.reshape(128, depth)
+            parts.append(everyone[at + (lines, slice(None))].reshape(128, everyone.shape[4]))
             rows.append(pl.ds(pl.multiple_of(128 * (8 * colour + 4 * h + q), 128), 128))
-        count = x_pad.shape[0]
-        high, low = split(x_pad[...])
+        count = 128 * len(parts)
+        high, low = split(jnp.concatenate(parts, axis=0))
         both = jnp.concatenate([high, low], axis=0)
         step = 256
         for n in range(width // step):
@@ -311,119 +311,164 @@
             device_id_type=MESH,
         )
 
-    tiles = width // TILE
-
-    def optimize(iteration, carry):
-        copies = Copies(pos, send_sems, recv_sems, FRAME_COPIES)
-
-        def look_ahead(n, carry):
-            at = pl.ds(pl.multiple_of(n * TILE, TILE), TILE)
-            high, low = split((w_ref[:, at] + MOMENTUM * v_ref[:, at]) * scale)
-            a_stack[:classes, at] = high
-            a_stack[CLASS_PAD : CLASS_PAD + classes, at] = low
-            return carry
-
-        lax.fori_loop(0, tiles, look_ahead, 0)
-
-        def score(n, carry):
-            at = pl.ds(pl.multiple_of(n * TILE, TILE), TILE)
-            both = mul_flipped(a_stack[...], f_high[at, :])
-            low = mul_flipped(a_stack[:CLASS_PAD, :], f_low[at, :])
-            scores = both[:CLASS_PAD] + both[CLASS_PAD:] + low
-            for k in range(TILE // 128):
-                part = scores[:, 128 * k : 128 * (k + 1)].reshape(4, UNIT, 128)
-                p_ref[pl.ds(4 * (n * (TILE // 128) + k), 4)] = part
-            return carry
-
-        def residuals(block, carry):
-            row = lax.broadcasted_iota(jnp.int32, (CLASS_PAD, 128), 0)
-            scores = total[pl.ds(4 * block, 4)].reshape(CLASS_PAD, 128)
-            scores = jnp.where(row < classes, scores, -jnp.inf)
-            exponent = jnp.exp(scores - jnp.max(scores, axis=0, keepdims=True))
-            probability = exponent / jnp.sum(exponent, axis=0, keepdims=True)
-            label = labels_ref[pl.ds(block, 1), :]
-            residual = (probability - jnp.where(row == label, 1.0, 0.0)) * scale
-            at = pl.ds(pl.multiple_of(block * 128, 128), 128)
-            r_stack[:CLASS_PAD, at], r_stack[CLASS_PAD:, at] = split(residual)
-            return carry
-
-        def gradient(chunk, n, carry):
-            at = pl.ds(pl.multiple_of(n * TILE, TILE), TILE)
-            rows = pl.ds(chunk * (frames // CHUNKS), frames // CHUNKS)
-            both = mul(r_stack[:, rows], f_high[rows, at])
-            value = both[:CLASS_PAD] + both[CLASS_PAD:]
-            value = value + mul(r_stack[:CLASS_PAD, rows], f_low[rows, at])
-            if chunk == 0:
-                g_ref[n] = value
-            else:
-                g_ref[n] = g_ref[n] + value
-            if chunk == CHUNKS - 1:
-                exchange(iteration, n).start()
-            return carry
-
-        def streams(chunk):
-            return [
-                sum_chunk(
-                    copies, chunk, colour, p_ref, total, wide, kept, narrow, unit, others
-                )
-                for colour in range(3)
-            ]
-
-        per_chunk = frames // TILE // CHUNKS
-        lax.fori_loop(0, per_chunk, score, 0)
-        early = advance_all(streams(0))
-        lax.fori_loop(per_chunk, 2 * per_chunk, score, 0)
-        late = advance_all(streams(1))
+    def look_ahead(momentum, n, carry):
+        at = pl.ds(pl.multiple_of(n * TILE, TILE), TILE)
+        high, low = split((w_ref[:, at] + momentum * v_ref[:, at]) * scale)
+        a_stack[:classes, at] = high
+        a_stack[CLASS_PAD : CLASS_PAD + classes, at] = low
+        return carry
+
+    def score(out_ref, n, carry):
+        at = pl.ds(pl.multiple_of(n * TILE, TILE), TILE)
+        both = mul_flipped(a_stack[...], f_high[at, :])
+        low = mul_flipped(a_stack[:CLASS_PAD, :], f_low[at, :])
+        scores = both[:CLASS_PAD] + both[CLASS_PAD:] + low
+        for k in range(TILE // 128):
+            part = scores[:, 128 * k : 128 * (k + 1)].reshape(4, UNIT, 128)
+            out_ref[pl.ds(4 * (n * (TILE // 128) + k), 4)] = part
+        return carry
+
+    def residuals(block, carry):
+        row = lax.broadcasted_iota(jnp.int32, (CLASS_PAD, 128), 0)
+        scores = total[pl.ds(4 * block, 4)].reshape(CLASS_PAD, 128)
+        scores = jnp.where(row < classes, scores, -jnp.inf)
+        exponent = jnp.exp(scores - jnp.max(scores, axis=0, keepdims=True))
+        probability = exponent / jnp.sum(exponent, axis=0, keepdims=True)
+        label = labels_ref[pl.ds(block, 1), :]
+        residual = (probability - jnp.where(row == label, 1.0, 0.0)) * scale
+        at = pl.ds(pl.multiple_of(block * 128, 128), 128)
+        r_stack[:CLASS_PAD, at], r_stack[CLASS_PAD:, at] = split(residual)
+        return carry
+
+    def gradient(iteration, chunk, n, carry):
+        at = pl.ds(pl.multiple_of(n * TILE, TILE), TILE)
+        rows = pl.ds(chunk * (frames // CHUNKS), frames // CHUNKS)
+        both = mul(r_stack[:, rows], f_high[rows, at])
+        value = both[:CLASS_PAD] + both[CLASS_PAD:]
+        value = value + mul(r_stack[:CLASS_PAD, rows], f_low[rows, at])
+        if chunk == 0:
+            g_ref[n] = value
+        else:
+            g_ref[n] = g_ref[n] + value
+        if chunk == CHUNKS - 1:
+            exchange(iteration, n).start()
+        return carry
+
+    def streams(chunk):
+        return [
+            sum_chunk(copies, chunk, colour, p_ref, total, wide, kept, narrow, unit, others)
+            for colour in range(3)
+        ]
+
+    def finish_step(iteration, early, late, pending):
         while early:
             early = advance_all(early)
             if early:
                 late = advance_all(late)
+            if pending:
+                pending.pop(0)()
         blocks = frames // 128 // CHUNKS
+        for work in pending:
+            work()
         lax.fori_loop(0, blocks, residuals, 0)
         late = advance_all(late)
-        lax.fori_loop(0, tiles, functools.partial(gradient, 0), 0)
+        lax.fori_loop(0, tiles, functools.partial(gradient, iteration, 0), 0)
         while late:
             late = advance_all(late)
         lax.fori_loop(blocks, 2 * blocks, residuals, 0)
-        lax.fori_loop(0, tiles, functools.partial(gradient, 1), 0)
-
+        lax.fori_loop(0, tiles, functools.partial(gradient, iteration, 1), 0)
+
+    def sum_squares(iteration, stacked):
         summed = jnp.zeros((8, TILE), jnp.float32)
         for n in range(tiles):
             exchange(iteration, n).wait_recv()
             value = g_ref[n] + g_other[iteration, n]
+            if stacked:
+                at = pl.ds(n * TILE, TILE)
+                a_stack[:CLASS_PAD, at], a_stack[CLASS_PAD:, at] = split(value * scale)
             value = value * value
             summed = summed + jnp.sum(value.reshape(CLASS_PAD // 8, 8, TILE), axis=0)
         squares[0] = jnp.sum(
             jnp.stack([summed[:, 128 * k : 128 * (k + 1)] for k in range(TILE // 128)]), axis=0
         )
+
+    def sum_over_chips():
         for stage, dim in enumerate("zxy"):
             sent = [
                 copies.send(squares.at[stage], square_parts.at[stage, slot], dim, step)
                 for slot, step in enumerate((2, 1, 3))
             ]
+            yield
             for copy in sent:
                 copy.wait_recv()
             squares[stage + 1] = (squares[stage] + square_parts[stage, 0]) + (
                 square_parts[stage, 1] + square_parts[stage, 2]
             )
+
+    def rate():
         square_sum = jnp.sum(squares[3], axis=(0, 1), keepdims=True)
-        rate = STEP_RATE / jnp.sqrt(square_sum / count_all + EPSILON)
-
-        def update(n, carry):
-            at = pl.ds(pl.multiple_of(n * TILE, TILE), TILE)
-            value = g_ref[n, :classes] + g_other[iteration, n, :classes]
-            speed = MOMENTUM * v_ref[:, at] - rate * value
-            v_ref[:, at] = speed
-            w_ref[:, at] = w_ref[:, at] + speed
-            return carry
-
-        lax.fori_loop(0, tiles, update, 0)
-        copies.wait_sends()
-        for n in range(tiles):
-            exchange(iteration, n).wait_send()
-        return carry
-
-    lax.fori_loop(0, ITERS, optimize, 0)
+        return STEP_RATE / jnp.sqrt(square_sum / count_all + EPSILON)
+
+    def update(iteration, step_rate, n, carry):
+        at = pl.ds(pl.multiple_of(n * TILE, TILE), TILE)
+        value = g_ref[n, :classes] + g_other[iteration, n, :classes]
+        speed = MOMENTUM * v_ref[:, at] - step_rate * value
+        v_ref[:, at] = speed
+        w_ref[:, at] = w_ref[:, at] + speed
+        return carry
+
+    def loop(first, last, body):
+        lax.fori_loop(first, last, body, 0)
+
+    tiles = width // TILE
+    score_tiles = frames // TILE
+    half = score_tiles // CHUNKS
+
+    copies = Copies(pos, send_sems, recv_sems, FRAME_COPIES)
+    loop(0, tiles, functools.partial(look_ahead, MOMENTUM))
+    loop(0, half, functools.partial(score, p_ref))
+    early = advance_all(streams(0))
+    loop(half, score_tiles, functools.partial(score, p_ref))
+    late = advance_all(streams(1))
+    loop(0, tiles, functools.partial(look_ahead, MOMENTUM * (1.0 + MOMENTUM)))
+    pending = [
+        functools.partial(loop, n, n + 1, functools.partial(score, p_next))
+        for n in range(score_tiles)
+    ]
+    finish_step(0, early, late, pending)
+
+    copies.wait_sends()
+    sum_squares(0, True)
+    travel = sum_over_chips()
+    for n in range(score_tiles):
+        if n % 2 == 0:
+            next(travel)
+        loop(n, n + 1, functools.partial(score, p_ref))
+    advance_all([travel])
+    step_rate = rate()
+    copies.wait_sends()
+    for n in range(tiles):
+        exchange(0, n).wait_send()
+    copies = Copies(pos, send_sems, recv_sems, FRAME_COPIES)
+
+    def combine(u, carry):
+        p_ref[u] = p_next[u] - ((1.0 + MOMENTUM) * step_rate) * p_ref[u]
+        return carry
+
+    units = p_ref.shape[0]
+    loop(0, units // CHUNKS, combine)
+    early = advance_all(streams(0))
+    loop(units // CHUNKS, units, combine)
+    late = advance_all(streams(1))
+    pending = [functools.partial(loop, 0, tiles, functools.partial(update, 0, step_rate))]
+    finish_step(1, early, late, pending)
+    sum_squares(1, False)
+    for _ in sum_over_chips():
+        pass
+    loop(0, tiles, functools.partial(update, 1, rate()))
+    copies.wait_sends()
+    for n in range(tiles):
+        exchange(1, n).wait_send()
 
 
 def regroup(labels):
@@ -452,14 +497,15 @@
         in_specs=[anywhere, vmem, anywhere, vmem, anywhere, anywhere],
         out_specs=[vmem, vmem],
         scratch_shapes=[
-            pltpu.VMEM((4, 4, 4) + frames.shape, f32),
+            pltpu.VMEM(frames.shape, f32),
+            pltpu.VMEM((4, 4, 4, frames.shape[0], 512), f32),
             pltpu.VMEM((depth, width), f32),
             pltpu.VMEM((512, width), bf16),
             pltpu.VMEM((512, width), bf16),
-            pltpu.VMEM((384, 512), f32),
             pltpu.VMEM((count, width), bf16),
             pltpu.VMEM((count, width), bf16),
             pltpu.VMEM((2 * CLASS_PAD, width), bf16),
+            pltpu.VMEM((units, UNIT, 128), f32),
             pltpu.VMEM((units, UNIT, 128), f32),
             pltpu.VMEM((units, UNIT, 128), f32),
             pltpu.VMEM((colours, 3, 4, UNIT, 128), f32),

time: 179 us -> 170 us (0.950)
  Pallas kernels: 172 us -> 163 us
    pallas_call x1, Pallas kernels: 172 us -> 163 us  [on_device(): pl.pallas_call(functools.partial(kernel, scale, feat_count * classes), ou...]
where the time goes in v3:
time: 170 us
  Pallas kernels  163 us (96%)
  local copies, waits for them, and re-layouts  5.04 us (3%)
    pallas_call x1, Pallas kernels, on_device(): pl.pallas_call(functools.partial(kernel, scale, feat_count * classes), ou...  163 us
    unnamed x4, local copies, waits for them, and re-layouts  3.58 us

profile of v3, /device:TPU:0, one launch (start us, length us, event | category | flops | bytes accessed | tf_op | source)
XLA Modules:
  0.0 169.8 jit_solution(5291886998701594125)
XLA Ops:
  0.6 1.0 reshape.19
  1.7 0.1 slice_bitcast_fusion.2
  1.8 0.1 reshape.20
  1.9 0.1 reshape.22
  2.0 0.1 reshape.21
  2.1 0.6 pad_add_fusion.labels_ref
  2.7 163.4 %optimize.1 = (f32[147,2048]{1,0:T(8,128)}, f32[147,2048]{1,0:T(8,128)}) custom-call(f32[48,440]{1,0:T(8,128)} %x_hbm.1, s32[24,128]{1,0:T(8,128)} %pad_add_fusion.labels_ref, f32[440,2048]{1,0:T(8,128)} %proj_hbm.1, f32[1,2048]{1,0:T(1,128)} %bitcast.21, f32[147,2048]{1,0:T(8,128)} %bitcast.17, f32[147,2048]{1,0:T(8,128)} %bitcast.18), custom_call_target="tpu_custom_call" | custom-call | tf_op jit(solution)/shard_map/optimize/pallas_call | solution.py:494
  166.2 0.0 copy-start
  166.2 2.5 %copy.15 = f32[2048,147]{0,1:T(8,128)} copy(f32[2048,147]{0,1:T(8,128)} %bitcast.20) | data formatting | bytes 2408448
  168.7 0.0 copy-done
  168.7 1.0 copy.16
  (3 shorter events, 0.1 us)
Async XLA Ops:
  166.2 2.6 %copy-start = (f32[147,2048]{1,0:T(8,128)S(1)}, f32[147,2048]{1,0:T(8,128)}, u32[]{:S(2)}) copy-start(f32[147,2048]{1,0:T(8,128)} %get-tuple-element.5) | copy-start | bytes 3612676

commit v4 on v3

--- a/solution.py
+++ b/solution.py
@@ -174,7 +174,7 @@
 
 def kernel(
     scale, count_all, x_hbm, labels_ref, proj_hbm, phase_ref, w_hbm, v_hbm, w_ref, v_ref,
-    x_ref, everyone, proj_ref, p_high, p_low, f_high, f_low, a_stack, p_ref, p_next, total,
+    label_rows, x_ref, everyone, proj_ref, p_high, p_low, f_high, f_low, a_stack, p_ref, p_next, total,
     wide, kept, narrow, unit, others, r_stack, g_ref, g_other, squares, square_parts,
     send_sems, recv_sems, pair_send, pair_recv, load_sems,
 ):
@@ -330,12 +330,13 @@
 
     def residuals(block, carry):
         row = lax.broadcasted_iota(jnp.int32, (CLASS_PAD, 128), 0)
+        number = row.astype(jnp.float32)
         scores = total[pl.ds(4 * block, 4)].reshape(CLASS_PAD, 128)
         scores = jnp.where(row < classes, scores, -jnp.inf)
         exponent = jnp.exp(scores - jnp.max(scores, axis=0, keepdims=True))
         probability = exponent / jnp.sum(exponent, axis=0, keepdims=True)
-        label = labels_ref[pl.ds(block, 1), :]
-        residual = (probability - jnp.where(row == label, 1.0, 0.0)) * scale
+        label = label_rows[pl.ds(block, 1), :]
+        residual = (probability - jnp.where(number == label, 1.0, 0.0)) * scale
         at = pl.ds(pl.multiple_of(block * 128, 128), 128)
         r_stack[:CLASS_PAD, at], r_stack[CLASS_PAD:, at] = split(residual)
         return carry
@@ -417,6 +418,32 @@
         w_ref[:, at] = w_ref[:, at] + speed
         return carry
 
+    def order_labels():
+        groups = frames // 8
+        held = labels_ref[...].astype(jnp.float32)
+        held = jnp.concatenate([held, jnp.zeros((128 - held.shape[0], 128), jnp.float32)], axis=0)
+        group = lax.broadcasted_iota(jnp.int32, (groups, 128), 0)
+        lane = lax.broadcasted_iota(jnp.int32, (groups, 128), 1)
+        picks = jnp.where((group >> 4) == lane, 1.0, 0.0).astype(jnp.bfloat16)
+        spread = mul(picks, held.astype(jnp.bfloat16))
+        spread = jnp.where((lane >> 3) == (group & 15), spread, 0.0).astype(jnp.bfloat16)
+        line = lax.broadcasted_iota(jnp.int32, (128, 128), 0)
+        column = lax.broadcasted_iota(jnp.int32, (128, 128), 1)
+        same = jnp.where((line & 7) == (column & 7), 1.0, 0.0).astype(jnp.bfloat16)
+        spread = mul(spread, same)
+        place = lane >> 3
+        for colour in range(3):
+            for h in range(2):
+                for q in range(4):
+                    device = (
+                        16 * q + place,
+                        4 * place + q,
+                        16 * (place >> 2) + 4 * q + (place & 3),
+                    )[colour]
+                    chosen = jnp.where(group == 6 * device + 2 * colour + h, spread, 0.0)
+                    block = 8 * colour + 4 * h + q
+                    label_rows[block : block + 1, :] = jnp.sum(chosen, axis=0, keepdims=True)
+
     def loop(first, last, body):
         lax.fori_loop(first, last, body, 0)
 
@@ -435,14 +462,13 @@
         functools.partial(loop, n, n + 1, functools.partial(score, p_next))
         for n in range(score_tiles)
     ]
-    finish_step(0, early, late, pending)
+    finish_step(0, early, late, [order_labels] + pending)
 
     copies.wait_sends()
     sum_squares(0, True)
     travel = sum_over_chips()
-    for n in range(score_tiles):
-        if n % 2 == 0:
-            next(travel)
+    for n in range(half):
+        next(travel)
         loop(n, n + 1, functools.partial(score, p_ref))
     advance_all([travel])
     step_rate = rate()
@@ -458,6 +484,7 @@
     units = p_ref.shape[0]
     loop(0, units // CHUNKS, combine)
     early = advance_all(streams(0))
+    loop(half, score_tiles, functools.partial(score, p_ref))
     loop(units // CHUNKS, units, combine)
     late = advance_all(streams(1))
     pending = [functools.partial(loop, 0, tiles, functools.partial(update, 0, step_rate))]
@@ -469,14 +496,6 @@
     copies.wait_sends()
     for n in range(tiles):
         exchange(1, n).wait_send()
-
-
-def regroup(labels):
-    parts = labels.reshape(4, 4, 4, 3, 2, 8)
-    orders = ((3, 0, 1, 2, 4), (3, 2, 0, 1, 4), (3, 1, 0, 2, 4))
-    return jnp.concatenate(
-        [parts[:, :, :, c].transpose(order).reshape(8, 128) for c, order in enumerate(orders)]
-    )
 
 
 def on_device(frames, labels, proj, phase, class_weights, velocity):
@@ -497,6 +516,7 @@
         in_specs=[anywhere, vmem, anywhere, vmem, anywhere, anywhere],
         out_specs=[vmem, vmem],
         scratch_shapes=[
+            pltpu.VMEM((count // 128, 128), f32),
             pltpu.VMEM(frames.shape, f32),
             pltpu.VMEM((4, 4, 4, frames.shape[0], 512), f32),
             pltpu.VMEM((depth, width), f32),
@@ -528,7 +548,7 @@
             collective_id=0, has_side_effects=True, vmem_limit_bytes=VMEM_LIMIT
         ),
         name="optimize",
-    )(frames, regroup(labels), proj, phase.reshape(1, width), class_weights.T, velocity.T)
+    )(frames, labels.reshape(count // 128, 128), proj, phase.reshape(1, width), class_weights.T, velocity.T)
     return weights.T, speed.T
 
 

time: 170 us -> 171 us (level)
  Pallas kernels: 163 us -> 166 us
    pallas_call x1, Pallas kernels: 163 us -> 166 us  [on_device(): pl.pallas_call(functools.partial(kernel, scale, feat_count * classes), ou...]
where the time goes in v4:
time: 171 us; the launch traced here: 170 us
  Pallas kernels  166 us (97%)
  local copies, waits for them, and re-layouts  3.58 us (2%)
    pallas_call x1, Pallas kernels, on_device(): pl.pallas_call(functools.partial(kernel, scale, feat_count * classes), ou...  166 us
    unnamed x4, local copies, waits for them, and re-layouts  3.58 us

profile of v4, /device:TPU:0, one launch (start us, length us, event | category | flops | bytes accessed | tf_op | source)
XLA Modules:
  0.0 170.3 jit_solution(12751607224469494440)
XLA Ops:
  0.6 166.1 %optimize.1 = (f32[147,2048]{1,0:T(8,128)}, f32[147,2048]{1,0:T(8,128)}) custom-call(f32[48,440]{1,0:T(8,128)} %x_hbm.1, s32[24,128]{1,0:T(8,128)} %bitcast.10, f32[440,2048]{1,0:T(8,128)} %proj_hbm.1, f32[1,2048]{1,0:T(1,128)} %bitcast.11, f32[147,2048]{1,0:T(8,128)} %bitcast.6, f32[147,2048]{1,0:T(8,128)} %bitcast.7), custom_call_target="tpu_custom_call" | custom-call | tf_op jit(solution)/shard_map/optimize/pallas_call | solution.py:513
  166.7 0.0 copy-start
  166.8 2.5 %copy.10 = f32[2048,147]{0,1:T(8,128)} copy(f32[2048,147]{0,1:T(8,128)} %bitcast.9) | data formatting | bytes 2408448
  169.3 0.0 copy-done
  169.3 1.0 copy.11
Async XLA Ops:
  166.7 2.6 %copy-start = (f32[147,2048]{1,0:T(8,128)S(1)}, f32[147,2048]{1,0:T(8,128)}, u32[]{:S(2)}) copy-start(f32[147,2048]{1,0:T(8,128)} %get-tuple-element.5) | copy-start | bytes 3612676

commit v5 on v3

--- a/solution.py
+++ b/solution.py
@@ -174,7 +174,7 @@
 
 def kernel(
     scale, count_all, x_hbm, labels_ref, proj_hbm, phase_ref, w_hbm, v_hbm, w_ref, v_ref,
-    x_ref, everyone, proj_ref, p_high, p_low, f_high, f_low, a_stack, p_ref, p_next, total,
+    label_rows, x_ref, everyone, proj_ref, p_high, p_low, f_high, f_low, a_stack, p_ref, p_next, total,
     wide, kept, narrow, unit, others, r_stack, g_ref, g_other, squares, square_parts,
     send_sems, recv_sems, pair_send, pair_recv, load_sems,
 ):
@@ -241,10 +241,38 @@
         load_w.wait()
         load_v.wait()
 
+    def order_labels():
+        groups = frames // 8
+        held = labels_ref[...].astype(jnp.float32)
+        held = jnp.concatenate([held, jnp.zeros((128 - held.shape[0], 128), jnp.float32)], axis=0)
+        group = lax.broadcasted_iota(jnp.int32, (groups, 128), 0)
+        lane = lax.broadcasted_iota(jnp.int32, (groups, 128), 1)
+        picks = jnp.where((group >> 4) == lane, 1.0, 0.0).astype(jnp.bfloat16)
+        spread = mul(picks, held.astype(jnp.bfloat16))
+        spread = jnp.where((lane >> 3) == (group & 15), spread, 0.0).astype(jnp.bfloat16)
+        line = lax.broadcasted_iota(jnp.int32, (128, 128), 0)
+        column = lax.broadcasted_iota(jnp.int32, (128, 128), 1)
+        same = jnp.where((line & 7) == (column & 7), 1.0, 0.0).astype(jnp.bfloat16)
+        spread = mul(spread, same)
+        place = lane >> 3
+        for colour in range(3):
+            for h in range(2):
+                for q in range(4):
+                    device = (
+                        16 * q + place,
+                        4 * place + q,
+                        16 * (place >> 2) + 4 * q + (place & 3),
+                    )[colour]
+                    chosen = jnp.where(group == 6 * device + 2 * colour + h, spread, 0.0)
+                    block = 8 * colour + 4 * h + q
+                    label_rows[block : block + 1, :] = jnp.sum(chosen, axis=0, keepdims=True)
+
     streams = advance_all([near(colour) for colour in range(3)])
     prepare_proj()
     streams = advance_all(streams)
     prepare_rest()
+    streams = advance_all(streams)
+    order_labels()
     while streams:
         streams = advance_all(streams)
 
@@ -330,12 +358,13 @@
 
     def residuals(block, carry):
         row = lax.broadcasted_iota(jnp.int32, (CLASS_PAD, 128), 0)
+        number = row.astype(jnp.float32)
         scores = total[pl.ds(4 * block, 4)].reshape(CLASS_PAD, 128)
         scores = jnp.where(row < classes, scores, -jnp.inf)
         exponent = jnp.exp(scores - jnp.max(scores, axis=0, keepdims=True))
         probability = exponent / jnp.sum(exponent, axis=0, keepdims=True)
-        label = labels_ref[pl.ds(block, 1), :]
-        residual = (probability - jnp.where(row == label, 1.0, 0.0)) * scale
+        label = label_rows[pl.ds(block, 1), :]
+        residual = (probability - jnp.where(number == label, 1.0, 0.0)) * scale
         at = pl.ds(pl.multiple_of(block * 128, 128), 128)
         r_stack[:CLASS_PAD, at], r_stack[CLASS_PAD:, at] = split(residual)
         return carry
@@ -428,7 +457,9 @@
     loop(0, tiles, functools.partial(look_ahead, MOMENTUM))
     loop(0, half, functools.partial(score, p_ref))
     early = advance_all(streams(0))
-    loop(half, score_tiles, functools.partial(score, p_ref))
+    loop(half, score_tiles - 1, functools.partial(score, p_ref))
+    early = advance_all(early)
+    loop(score_tiles - 1, score_tiles, functools.partial(score, p_ref))
     late = advance_all(streams(1))
     loop(0, tiles, functools.partial(look_ahead, MOMENTUM * (1.0 + MOMENTUM)))
     pending = [
@@ -440,9 +471,8 @@
     copies.wait_sends()
     sum_squares(0, True)
     travel = sum_over_chips()
-    for n in range(score_tiles):
-        if n % 2 == 0:
-            next(travel)
+    for n in range(half):
+        next(travel)
         loop(n, n + 1, functools.partial(score, p_ref))
     advance_all([travel])
     step_rate = rate()
@@ -458,6 +488,9 @@
     units = p_ref.shape[0]
     loop(0, units // CHUNKS, combine)
     early = advance_all(streams(0))
+    loop(half, score_tiles - 1, functools.partial(score, p_ref))
+    early = advance_all(early)
+    loop(score_tiles - 1, score_tiles, functools.partial(score, p_ref))
     loop(units // CHUNKS, units, combine)
     late = advance_all(streams(1))
     pending = [functools.partial(loop, 0, tiles, functools.partial(update, 0, step_rate))]
@@ -469,14 +502,6 @@
     copies.wait_sends()
     for n in range(tiles):
         exchange(1, n).wait_send()
-
-
-def regroup(labels):
-    parts = labels.reshape(4, 4, 4, 3, 2, 8)
-    orders = ((3, 0, 1, 2, 4), (3, 2, 0, 1, 4), (3, 1, 0, 2, 4))
-    return jnp.concatenate(
-        [parts[:, :, :, c].transpose(order).reshape(8, 128) for c, order in enumerate(orders)]
-    )
 
 
 def on_device(frames, labels, proj, phase, class_weights, velocity):
@@ -497,6 +522,7 @@
         in_specs=[anywhere, vmem, anywhere, vmem, anywhere, anywhere],
         out_specs=[vmem, vmem],
         scratch_shapes=[
+            pltpu.VMEM((count // 128, 128), f32),
             pltpu.VMEM(frames.shape, f32),
             pltpu.VMEM((4, 4, 4, frames.shape[0], 512), f32),
             pltpu.VMEM((depth, width), f32),
@@ -528,7 +554,7 @@
             collective_id=0, has_side_effects=True, vmem_limit_bytes=VMEM_LIMIT
         ),
         name="optimize",
-    )(frames, regroup(labels), proj, phase.reshape(1, width), class_weights.T, velocity.T)
+    )(frames, labels.reshape(count // 128, 128), proj, phase.reshape(1, width), class_weights.T, velocity.T)
     return weights.T, speed.T
 
 

time: 170 us -> 168 us (0.988)
  no operation moved by 1% of the time
where the time goes in v5:
time: 168 us
  Pallas kernels  163 us (97%)
  local copies, waits for them, and re-layouts  3.58 us (2%)
    pallas_call x1, Pallas kernels, on_device(): pl.pallas_call(functools.partial(kernel, scale, feat_count * classes), ou...  163 us
    unnamed x4, local copies, waits for them, and re-layouts  3.58 us

profile of v5, /device:TPU:0, one launch (start us, length us, event | category | flops | bytes accessed | tf_op | source)
XLA Modules:
  0.0 167.6 jit_solution(17215386165010957393)
XLA Ops:
  0.6 163.3 %optimize.1 = (f32[147,2048]{1,0:T(8,128)}, f32[147,2048]{1,0:T(8,128)}) custom-call(f32[48,440]{1,0:T(8,128)} %x_hbm.1, s32[24,128]{1,0:T(8,128)} %bitcast.10, f32[440,2048]{1,0:T(8,128)} %proj_hbm.1, f32[1,2048]{1,0:T(1,128)} %bitcast.11, f32[147,2048]{1,0:T(8,128)} %bitcast.6, f32[147,2048]{1,0:T(8,128)} %bitcast.7), custom_call_target="tpu_custom_call" | custom-call | tf_op jit(solution)/shard_map/optimize/pallas_call | solution.py:519
  164.0 0.0 copy-start
  164.0 2.5 %copy.10 = f32[2048,147]{0,1:T(8,128)} copy(f32[2048,147]{0,1:T(8,128)} %bitcast.9) | data formatting | bytes 2408448
  166.5 0.0 copy-done
  166.5 1.0 copy.11
Async XLA Ops:
  164.0 2.6 %copy-start = (f32[147,2048]{1,0:T(8,128)S(1)}, f32[147,2048]{1,0:T(8,128)}, u32[]{:S(2)}) copy-start(f32[147,2048]{1,0:T(8,128)} %get-tuple-element.5) | copy-start | bytes 3612676
